TPU v7x, 512 devices: a whole 4x8x8 slice. The times are simulated.
512 devices in a mesh: rows: 64 (over z, y), heads: 8 (over x, core).
Axes of the slice: x: 4, y: 8, z: 8, core: 2. Of those that a mesh axis runs over, the one named last changes fastest.
Arguments:
- queries: bfloat16 [8192, 8192], P('rows', 'heads'), may hold values from -128 to 128
- new_keys: bfloat16 [8192, 1024], P('rows', 'heads'), may hold values from -8 to 8
- new_values: bfloat16 [8192, 1024], P('rows', 'heads'), may hold values from -6 to 6
- library_keys: bfloat16 [1024, 128, 1024], P('rows', None, 'heads'), may hold values from -6 to 6
- library_values: bfloat16 [1024, 128, 1024], P('rows', None, 'heads'), may hold values from -6 to 6
- module_owner: int32 [64, 16], P('rows'), may hold values from 0 to 63, as said below
- module_page: int32 [64, 16], P('rows'), may hold values from 0 to 15
- module_count: int32 [64], P('rows'), may hold values from 1 to 16, 896 in all
Outputs:
- attended: bfloat16 [8192, 8192], P(('rows', 'heads'))
Inputs may be any that keep to these rules, and one draw needn't show every extreme that they name: `module_owner`: among the 16 listed pages of the requests of one index of rows, live or not, no owner is named more than 2 times, and some owner exactly 2 times.
All inputs are finite; a program needn't handle non-finite values. No bound on the sum of `module_count` on one device may be relied on, other than what follows from the above.
Results may differ from a plain program's by a relative error of at most 0.0035.
Values may be sent and summed in bfloat16 or wider, within the bound.
A program may use at most 64 MiB of HBM per device.

v0:
```python
import math

import jax
import jax.numpy as jnp
from jax import lax
from jax.sharding import PartitionSpec as P

HD = 128
QH = 64
KVH = 8


def slot_plan(owners, pages, live_slot, rows_count, capacity):
    entries = owners.shape[0]
    position = jnp.arange(entries, dtype=jnp.int32)
    earlier = (
        (owners[:, None] == owners[None, :])
        & live_slot[:, None]
        & live_slot[None, :]
        & (position[None, :] < position[:, None])
    )
    ranking = jnp.sum(earlier.astype(jnp.int32), axis=1)
    slot_index = jnp.where(live_slot, owners * capacity + ranking, 0)
    matches = (
        slot_index[:, None] == jnp.arange(rows_count * capacity, dtype=jnp.int32)[None, :]
    ) & live_slot[:, None]
    requested = jnp.sum(jnp.where(matches, pages[:, None], 0), axis=0)
    return (slot_index, requested)


def attend_request(query_rows, keys_all, values_all, allowed, kv_local, group_size):
    new_len = query_rows.shape[0]
    score_scale = 1.0 / math.sqrt(HD)
    per_block = min(group_size, max(1, 512 // new_len))
    shaped = query_rows.reshape(new_len, kv_local, group_size, HD)
    blocks = []
    for head_start in range(0, group_size, per_block):
        query_block = shaped[:, 0, head_start : head_start + per_block, :]
        scores = (
            jnp.einsum("tgd,sd->gts", query_block, keys_all, preferred_element_type=jnp.float32)
            * score_scale
        )
        scores = jnp.where(allowed[None], scores, -1e30)
        row_max = jnp.max(scores, axis=2, keepdims=True)
        weights = jnp.where(allowed[None], jnp.exp(scores - row_max), 0.0)
        totals = jnp.sum(weights, axis=2)
        mixed_rows = jnp.einsum(
            "gts,sd->tgd",
            weights.astype(jnp.bfloat16),
            values_all,
            preferred_element_type=jnp.float32,
        )
        blocks.append(mixed_rows / jnp.transpose(totals)[:, :, None])
    pieces = [jnp.concatenate(blocks, axis=1)]
    return jnp.stack(pieces, axis=1).reshape(new_len, kv_local * group_size * HD)


def per_device(
    queries,
    new_keys,
    new_values,
    library_keys,
    library_values,
    module_owner,
    module_page,
    module_count,
):
    rows_count = lax.axis_size("rows")
    requests, module_max = module_owner.shape
    entries = requests * module_max
    capacity = max(2, -(-entries // rows_count))
    kv_features = new_keys.shape[1]
    kv_local = kv_features // HD
    group_size = QH // KVH
    new_len = queries.shape[0] // requests
    page_len = library_keys.shape[1]
    slots_live = jnp.arange(module_max, dtype=jnp.int32)[None, :] < module_count[:, None]
    slot_index, requested = slot_plan(
        module_owner.reshape(-1),
        module_page.reshape(-1),
        slots_live.reshape(-1),
        rows_count,
        capacity,
    )
    page_index = lax.all_to_all(
        requested.reshape(rows_count, capacity), "rows", split_axis=0, concat_axis=0, tiled=True
    )
    keys_in = lax.all_to_all(
        library_keys[page_index], "rows", split_axis=0, concat_axis=0, tiled=True
    ).reshape(rows_count * capacity, page_len, kv_features)[slot_index]
    keys_in = keys_in.reshape(requests, module_max * page_len, kv_features)
    values_in = lax.all_to_all(
        library_values[page_index], "rows", split_axis=0, concat_axis=0, tiled=True
    ).reshape(rows_count * capacity, page_len, kv_features)[slot_index]
    values_in = values_in.reshape(requests, module_max * page_len, kv_features)
    causal = jnp.arange(new_len)[None, :] <= jnp.arange(new_len)[:, None]
    library_live = jnp.repeat(slots_live[0], page_len)
    allowed = jnp.concatenate(
        [jnp.broadcast_to(library_live[None, :], (new_len, module_max * page_len)), causal], axis=1
    )
    keys_all = jnp.concatenate([keys_in[0], new_keys], axis=0)
    values_all = jnp.concatenate([values_in[0], new_values], axis=0)
    outputs = attend_request(queries, keys_all, values_all, allowed, kv_local, group_size)
    result = outputs.astype(jnp.bfloat16)
    return lax.all_to_all(result, "heads", split_axis=0, concat_axis=1, tiled=True)


def solution(mesh):
    placed = (
        P("rows", "heads"),
        P("rows", "heads"),
        P("rows", "heads"),
        P("rows", None, "heads"),
        P("rows", None, "heads"),
        P("rows", None),
        P("rows", None),
        P("rows"),
    )
    return jax.shard_map(
        per_device,
        mesh=mesh,
        in_specs=placed,
        out_specs=P(("rows", "heads"), None),
        check_vma=False,
    )
```

profile of v0, /device:TPU:112, one launch (start us, length us, event | category | flops | bytes accessed | tf_op | source)
XLA Modules:
  0.0 321.2 jit_solution(11225844853448301435)
XLA Ops:
  0.0 0.0 copy-start
  0.7 0.9 convert_reduce_fusion
  1.6 0.7 add_select_fusion
  2.3 0.7 select_reduce_fusion
  3.0 0.1 all_to_all.26
  3.2 23.0 %all_to_all.38 = s32[64,1,2]{2,1,0:T(1,128)S(1)} all-to-all(s32[64,1,2]{2,1,0:T(1,128)S(1)} %bitcast.146), channel_id=1, replica_groups=mesh['rows'=64,'heads'=8] {'rows'}, dimensions={0} | all-to-all | bytes 1024 | tf_op jit(solution)/shard_map/all_to_all | solution.py:85
  26.2 0.1 copy.49
  26.2 0.1 copy.50
  26.3 0.1 reshape.120
  26.5 0.0 copy-done
  26.5 3.1 gather_fusion.2
  29.6 0.0 copy-start.1
  29.6 9.6 %all-to-all-start.2 = ((bf16[64,2,128,128]{3,2,1,0:T(8,128)(2,1)}), bf16[64,2,128,128]{3,2,1,0:T(8,128)(2,1)}, u32[]{:S(2)}, u32[]{:S(2)}) async-start(bf16[64,2,128,128]{3,2,1,0:T(8,128)(2,1)} %bitcast.135), calls=%async_computation.2 | async-start | bytes 8388608 | tf_op jit(solution)/shard_map/all_to_all | solution.py:88
  39.2 0.0 copy-done.1
  39.2 3.1 gather_fusion
  42.3 130.3 %all-to-all-done.2 = bf16[64,2,128,128]{3,2,1,0:T(8,128)(2,1)} async-done(((bf16[64,2,128,128]{3,2,1,0:T(8,128)(2,1)}), bf16[64,2,128,128]{3,2,1,0:T(8,128)(2,1)}, u32[]{:S(2)}, u32[]{:S(2)}) %all-to-all-start.2) | async-done | bytes 4194336 | tf_op jit(solution)/shard_map/all_to_all | solution.py:88
  172.6 0.0 copy-start.3
  172.6 0.0 copy-start.2
  172.6 0.0 copy-start.4
  172.6 0.0 copy-start.5
  172.6 8.2 %all-to-all-start.1 = ((bf16[64,2,128,128]{3,2,1,0:T(8,128)(2,1)}), bf16[64,2,128,128]{3,2,1,0:T(8,128)(2,1)}, u32[]{:S(2)}, u32[]{:S(2)}) async-start(bf16[64,2,128,128]{3,2,1,0:T(8,128)(2,1)} %bitcast.134), calls=%async_computation.1 | async-start | bytes 8388608 | tf_op jit(solution)/shard_map/all_to_all | solution.py:92
  180.8 0.0 copy-done.3
  180.8 0.1 copy.52
  180.9 0.0 copy-done.2
  181.0 0.2 copy.53
  181.1 0.1 broadcast_bitcast_fusion
  181.2 0.0 copy-done.4
  181.3 2.1 pad_add_fusion
  183.3 2.8 gather_fusion.3
  186.2 0.0 copy-done.5
  186.2 1.9 fusion.67
  188.1 1.9 fusion.68
  190.1 111.4 %all-to-all-done.1 = bf16[64,2,128,128]{3,2,1,0:T(8,128)(2,1)} async-done(((bf16[64,2,128,128]{3,2,1,0:T(8,128)(2,1)}), bf16[64,2,128,128]{3,2,1,0:T(8,128)(2,1)}, u32[]{:S(2)}, u32[]{:S(2)}) %all-to-all-start.1) | async-done | bytes 4194336 | tf_op jit(solution)/shard_map/all_to_all | solution.py:92
  301.4 2.8 gather_fusion.1
  304.3 0.2 copy.62
  304.5 2.0 fusion.28
  306.5 2.0 fusion.31
  308.5 0.2 copy.58
  308.7 0.1 convert_element_type.17
  308.8 11.6 %all_to_all.39 = bf16[8,16,1024]{2,1,0:T(8,128)(2,1)S(1)} all-to-all(bf16[8,16,1024]{2,1,0:T(8,128)(2,1)S(1)} %convert_element_type.17), channel_id=1, replica_groups=mesh['rows'=64,'heads'=8] {'heads'}, dimensions={0} | all-to-all | bytes 524288 | tf_op jit(solution)/shard_map/all_to_all | solution.py:105
  320.5 0.7 copy.65
  (8 shorter events, 0.1 us)
Async XLA Ops:
  0.0 26.5 %copy-start = (bf16[16,128,128]{2,1,0:T(8,128)(2,1)S(1)}, bf16[16,128,128]{2,1,0:T(8,128)(2,1)}, u32[]{:S(2)}) copy-start(bf16[16,128,128]{2,1,0:T(8,128)(2,1)} %param.11) | copy-start | bytes 1572868
  29.6 9.6 %copy-start.1 = (bf16[16,128,128]{2,1,0:T(8,128)(2,1)S(1)}, bf16[16,128,128]{2,1,0:T(8,128)(2,1)}, u32[]{:S(2)}) copy-start(bf16[16,128,128]{2,1,0:T(8,128)(2,1)} %param.12) | copy-start | bytes 1572868
  29.6 143.0 %all-to-all-start.2 = ((bf16[64,2,128,128]{3,2,1,0:T(8,128)(2,1)}), bf16[64,2,128,128]{3,2,1,0:T(8,128)(2,1)}, u32[]{:S(2)}, u32[]{:S(2)}) async-start(bf16[64,2,128,128]{3,2,1,0:T(8,128)(2,1)} %bitcast.135), calls=%async_computation.2 | async-start | bytes 8388608 | tf_op jit(solution)/shard_map/all_to_all | solution.py:88
  172.6 8.3 %copy-start.3 = (bf16[128,128]{1,0:T(8,128)(2,1)S(1)}, bf16[128,128]{1,0:T(8,128)(2,1)}, u32[]{:S(2)}) copy-start(bf16[128,128]{1,0:T(8,128)(2,1)} %param.10) | copy-start | bytes 98308
  172.6 8.4 %copy-start.2 = (bf16[128,1024]{1,0:T(8,128)(2,1)S(1)}, bf16[128,1024]{1,0:T(8,128)(2,1)}, u32[]{:S(2)}) copy-start(bf16[128,1024]{1,0:T(8,128)(2,1)} %param.8) | copy-start | bytes 786436
  172.6 8.7 %copy-start.4 = (s32[1,16]{1,0:T(1,128)S(1)}, s32[1,16]{1,0:T(1,128)}, u32[]{:S(2)}) copy-start(s32[1,16]{1,0:T(1,128)} %param.13) | copy-start | bytes 196
  172.6 13.6 %copy-start.5 = (bf16[128,128]{1,0:T(8,128)(2,1)S(1)}, bf16[128,128]{1,0:T(8,128)(2,1)}, u32[]{:S(2)}) copy-start(bf16[128,128]{1,0:T(8,128)(2,1)} %param.9) | copy-start | bytes 98308
  172.6 128.9 %all-to-all-start.1 = ((bf16[64,2,128,128]{3,2,1,0:T(8,128)(2,1)}), bf16[64,2,128,128]{3,2,1,0:T(8,128)(2,1)}, u32[]{:S(2)}, u32[]{:S(2)}) async-start(bf16[64,2,128,128]{3,2,1,0:T(8,128)(2,1)} %bitcast.134), calls=%async_computation.1 | async-start | bytes 8388608 | tf_op jit(solution)/shard_map/all_to_all | solution.py:92
where the time goes:
time: 322 us; the launch traced here: 321 us
  waiting for transfers between devices  242 us (75%)
  blocking collectives  34.6 us (11%)
  starting transfers between devices  17.9 us (6%)
  local copies, waits for them, and re-layouts  13.9 us (4%)
  matrix products  7.85 us (2%)
  other arithmetic  4.46 us (1%)
    all_to_all x1, waiting for transfers between devices, per_device(): lax.all_to_all(library_keys[page_index], 'rows', split_axis=0, concat_axi...  130 us
    all_to_all x1, waiting for transfers between devices, per_device(): lax.all_to_all(library_values[page_index], 'rows', split_axis=0, concat_a...  111 us
    all_to_all x1, blocking collectives, per_device(): lax.all_to_all(requested.reshape(rows_count, capacity), 'rows', split_axi...  23 us
    all_to_all x1, blocking collectives, per_device(): lax.all_to_all(result, 'heads', split_axis=0, concat_axis=1, tiled=True)  11.6 us
    all_to_all x1, starting transfers between devices, per_device(): lax.all_to_all(library_keys[page_index], 'rows', split_axis=0, concat_axi...  9.61 us
    all_to_all x1, starting transfers between devices, per_device(): lax.all_to_all(library_values[page_index], 'rows', split_axis=0, concat_a...  8.24 us
  transfers between devices with their start and end apart: 2, of which 2 were waited for; matrix products, arithmetic and copies ran while one was open for 4% of the time, Pallas kernels for 0%

commit v1 on v0

v1 whole, which is shorter than its diff:
```python
import functools
import math

import jax
import jax.numpy as jnp
from jax import lax
from jax.experimental import pallas as pl
from jax.experimental.pallas import tpu as pltpu
from jax.sharding import PartitionSpec as P

HD = 128
QH = 64
KVH = 8
GROUP = QH // KVH
MESH = pl.DeviceIdType.MESH
LOG2E = 1.4426950408889634
FLOOR = -1e30


def place(side):
    row = lax.axis_index("rows")
    core = lax.rem(lax.axis_index("heads"), 2)
    z, y = row // side, lax.rem(row, side)
    u = (1 - core) * z + core * y
    w = (1 - core) * y + core * z
    return core, u, w


def row_of(core, u, w, side):
    return (1 - core) * (u * side + w) + core * (w * side + u)


def wrap(value, side):
    return lax.rem(value + 4 * side, side)


def gather_kernel(side, k_in, v_in, q_in, t_in, k_all, v_all, q_all, t_all, send, recv, local):
    core, u, w = place(side)
    half = side // 2
    tokens = q_in.shape[0]
    lib_at = [row_of(core, wrap(u + d, side), w, side) for d in (1, -1)]
    que_at = [row_of(core, u, wrap(w + d, side), side) for d in (1, -1)]

    barrier = pltpu.get_barrier_semaphore()
    for row in lib_at + que_at:
        pl.semaphore_signal(barrier, inc=1, device_id={"rows": row}, device_id_type=MESH)
    pl.semaphore_wait(barrier, 4)

    own = [
        pltpu.make_async_copy(k_in, k_all.at[u], local.at[0]),
        pltpu.make_async_copy(v_in, v_all.at[u], local.at[1]),
        pltpu.make_async_copy(q_in, q_all.at[w], local.at[2]),
        pltpu.make_async_copy(t_in, t_all.at[w], local.at[3]),
    ]

    def parts(dirn, step):
        last = step == half - 1
        sign = (1, -1)[dirn]
        u0, w0 = wrap(u - sign * step, side), wrap(w - sign * step, side)
        lib, que = lib_at[dirn], que_at[dirn]
        first = step == 0
        rows = pl.ds((0, tokens // 2)[dirn], tokens // 2)
        k = ((k_in if first else k_all.at[u0]), k_all.at[u0], lib, 0)
        v = ((v_in if first else v_all.at[u0]), v_all.at[u0], lib, 1)
        t = ((t_in if first else t_all.at[w0]), t_all.at[w0], que, 3)
        if last:
            q = (q_all.at[w0, rows], q_all.at[w0, rows], que, 2)
            return [q, k, t] if dirn == 0 else [q, v]
        q = ((q_in if first else q_all.at[w0]), q_all.at[w0], que, 2)
        return [t, q, k, v] if dirn == 0 else [t, q, v, k]

    started = {}
    waited = set()

    def start(dirn, step, part):
        src, dst, row, kind = part
        copy = pltpu.make_async_remote_copy(
            src_ref=src,
            dst_ref=dst,
            send_sem=send.at[dirn, step, kind],
            recv_sem=recv.at[dirn, step, kind],
            device_id={"rows": row},
            device_id_type=MESH,
        )
        copy.start()
        started[dirn, step, kind] = copy

    for step in range(half):
        lists = [parts(dirn, step) for dirn in (0, 1)]
        for place_in_list in range(4):
            for dirn in (0, 1):
                if place_in_list >= len(lists[dirn]):
                    continue
                part = lists[dirn][place_in_list]
                before = (dirn, step - 1, part[3])
                if step > 0:
                    started[before].wait_recv()
                    waited.add(before)
                start(dirn, step, part)
        if step == 0:
            for copy in own:
                copy.start()
    for key, copy in started.items():
        if key not in waited:
            copy.wait_recv()
    for copy in started.values():
        copy.wait_send()
    for copy in own:
        copy.wait()


def gather_lines(k, v, q, t, side):
    half = side // 2
    shapes = [jax.ShapeDtypeStruct((side,) + a.shape, a.dtype) for a in (k, v, q, t)]
    anywhere = pl.BlockSpec(memory_space=pl.ANY)
    return pl.pallas_call(
        functools.partial(gather_kernel, side),
        out_shape=shapes,
        in_specs=[anywhere] * 4,
        out_specs=[anywhere] * 4,
        scratch_shapes=[
            pltpu.SemaphoreType.DMA((2, half, 4)),
            pltpu.SemaphoreType.DMA((2, half, 4)),
            pltpu.SemaphoreType.DMA((4,)),
        ],
        compiler_params=pltpu.CompilerParams(
            collective_id=0, has_side_effects=True, vmem_limit_bytes=48 << 20
        ),
        name="gather_lines",
    )(k, v, q, t)


def partial_kernel(
    side, codes, where_ref, q_ref, nk_ref, nv_ref, k_hbm, v_hbm, acc_out, stat_out, kbuf, vbuf, ksem, vsem, acc, stat
):
    step = pl.program_id(0)
    core, w = where_ref[0], where_ref[1]
    slots = kbuf.shape[0] // side
    pages = k_hbm.shape[1]
    scale = LOG2E / math.sqrt(HD)
    tokens = q_ref.shape[1]
    rows = GROUP * tokens

    def entry(req, slot):
        code = codes[req, 0, slot]
        owner, page = code // pages, lax.rem(code, pages)
        z, y = owner // side, lax.rem(owner, side)
        line = (1 - core) * z + core * y
        cross = (1 - core) * y + core * z
        mine = jnp.logical_and(code >= 0, cross == w)
        return mine, line, page

    def copies(req, slot, line, page):
        at = req * slots + slot
        return (
            pltpu.make_async_copy(k_hbm.at[line, page], kbuf.at[at], ksem.at[at]),
            pltpu.make_async_copy(v_hbm.at[line, page], vbuf.at[at], vsem.at[at]),
        )

    @pl.when(step == 0)
    def _():
        @pl.loop(0, side * slots)
        def _(at):
            req, slot = at // slots, lax.rem(at, slots)
            mine, line, page = entry(req, slot)

            @pl.when(mine)
            def _():
                for copy in copies(req, slot, line, page):
                    copy.start()

    wide = 2 * tokens

    def chunk_q(c):
        j = 2 * c
        return jnp.concatenate(
            [q_ref[0, :, j * HD : (j + 1) * HD], q_ref[0, :, (j + 1) * HD : (j + 2) * HD]], axis=0
        )

    def scores(keys, c):
        return lax.dot_general(
            keys, chunk_q(c), (((1,), (1,)), ((), ())), preferred_element_type=jnp.float32
        )

    def mix(values, weights):
        return lax.dot_general(
            values, weights.astype(jnp.bfloat16), (((0,), (0,)), ((), ())), preferred_element_type=jnp.float32
        )

    @pl.when(step != w)
    def _():
        acc[...] = jnp.zeros_like(acc)
        stat[0:1] = jnp.full((1, rows), FLOOR, jnp.float32)
        stat[1:2] = jnp.zeros((1, rows), jnp.float32)

    @pl.when(step == w)
    def _():
        keys, values = nk_ref[...], nv_ref[...]
        for c in range(rows // wide):
            cols = slice(c * wide, (c + 1) * wide)
            raw = scores(keys, c)
            key_at = lax.broadcasted_iota(jnp.int32, raw.shape, 0)
            token_at = lax.rem(lax.broadcasted_iota(jnp.int32, raw.shape, 1), tokens)
            allowed = key_at <= token_at
            raw = jnp.where(allowed, raw, FLOOR)
            top = jnp.max(raw, axis=0, keepdims=True) * scale
            weights = jnp.where(allowed, jnp.exp2(raw * scale - top), 0.0)
            stat[0:1, cols] = top
            stat[1:2, cols] = jnp.sum(weights, axis=0, keepdims=True)
            acc[:, cols] = mix(values, weights)

    @pl.loop(0, slots)
    def _(slot):
        mine, line, page = entry(step, slot)

        @pl.when(mine)
        def _():
            for copy in copies(step, slot, line, page):
                copy.wait()
            at = step * slots + slot
            keys, values = kbuf[at], vbuf[at]
            for c in range(rows // wide):
                cols = slice(c * wide, (c + 1) * wide)
                raw = scores(keys, c)
                old = stat[0:1, cols]
                top = jnp.maximum(old, jnp.max(raw, axis=0, keepdims=True) * scale)
                weights = jnp.exp2(raw * scale - top)
                shrink = jnp.exp2(old - top)
                stat[0:1, cols] = top
                stat[1:2, cols] = stat[1:2, cols] * shrink + jnp.sum(weights, axis=0, keepdims=True)
                acc[:, cols] = acc[:, cols] * shrink + mix(values, weights)

    acc_out[0] = acc[...]
    stat_out[0] = stat[...]


def partials(codes, where, q_all, nk, nv, k_all, v_all, side):
    tokens = q_all.shape[1]
    rows = GROUP * tokens
    slots = 16
    page = k_all.shape[2:]
    whole = lambda a: pl.BlockSpec(a.shape, lambda i: (0,) * a.ndim)
    return pl.pallas_call(
        functools.partial(partial_kernel, side),
        grid=(side,),
        out_shape=[
            jax.ShapeDtypeStruct((side, HD, rows), jnp.float32),
            jax.ShapeDtypeStruct((side, 2, rows), jnp.float32),
        ],
        in_specs=[
            pl.BlockSpec(memory_space=pltpu.SMEM),
            pl.BlockSpec(memory_space=pltpu.SMEM),
            pl.BlockSpec((1, tokens, GROUP * HD), lambda i: (i, 0, 0)),
            whole(nk),
            whole(nv),
            pl.BlockSpec(memory_space=pl.ANY),
            pl.BlockSpec(memory_space=pl.ANY),
        ],
        out_specs=[
            pl.BlockSpec((1, HD, rows), lambda i: (i, 0, 0)),
            pl.BlockSpec((1, 2, rows), lambda i: (i, 0, 0)),
        ],
        scratch_shapes=[
            pltpu.VMEM((side * slots,) + page, jnp.bfloat16),
            pltpu.VMEM((side * slots,) + page, jnp.bfloat16),
            pltpu.SemaphoreType.DMA((side * slots,)),
            pltpu.SemaphoreType.DMA((side * slots,)),
            pltpu.VMEM((HD, rows), jnp.float32),
            pltpu.VMEM((2, rows), jnp.float32),
        ],
        compiler_params=pltpu.CompilerParams(vmem_limit_bytes=48 << 20),
        name="partials",
    )(codes, where, q_all, nk, nv, k_all, v_all)


def return_kernel(
    side, acc_hbm, stat_hbm, out, accs, stats, acc_send, stat_send, acc_recv, stat_recv, result, send, recv, load, xsend, xrecv, xlocal
):
    core, u, w = place(side)
    me = lax.axis_index("heads")
    peers = lax.axis_size("heads")
    half = side // 2
    rows = accs.shape[2]
    part = rows // 2
    tokens = result.shape[0]
    share = tokens // peers
    near = [row_of(core, u, wrap(w + d, side), side) for d in (1, -1)]

    barrier = pltpu.get_barrier_semaphore()
    for row in near:
        pl.semaphore_signal(barrier, inc=1, device_id={"rows": row}, device_id_type=MESH)
    for hop in range(1, peers):
        pl.semaphore_signal(
            barrier, inc=1, device_id={"heads": lax.rem(me + hop, peers)}, device_id_type=MESH
        )
    order = [half, half - 1, half + 1] + [d for k in range(half - 2, 0, -1) for d in (k, side - k)] + [0]
    loads = {}
    for d in order:
        target = wrap(w + d, side)
        loads[d] = [
            pltpu.make_async_copy(acc_hbm.at[target], accs.at[target], load.at[d, 0]),
            pltpu.make_async_copy(stat_hbm.at[target], stats.at[target], load.at[d, 1]),
        ]
        for copy in loads[d]:
            copy.start()
    loaded = set()
    pl.semaphore_wait(barrier, 1 + peers)

    def cols(c):
        return slice(c * part, (c + 1) * part)

    def far(dirn, c):
        return half if dirn == c else half - 1

    flights = {}

    def launch(dirn, c, k, acc_src, stat_src):
        copies = [
            pltpu.make_async_remote_copy(
                src_ref=src,
                dst_ref=dst,
                send_sem=send.at[dirn, c, k, kind],
                recv_sem=recv.at[dirn, c, k, kind],
                device_id={"rows": near[dirn]},
                device_id_type=MESH,
            )
            for kind, (src, dst) in enumerate(
                [(stat_src, stat_recv.at[dirn, c, k]), (acc_src, acc_recv.at[dirn, c, k])]
            )
        ]
        for copy in copies:
            copy.start()
        flights[dirn, c, k] = copies

    def merge(one, two):
        (acc_a, stat_a), (acc_b, stat_b) = one, two
        top = jnp.maximum(stat_a[0:1], stat_b[0:1])
        fa, fb = jnp.exp2(stat_a[0:1] - top), jnp.exp2(stat_b[0:1] - top)
        total = stat_a[1:2] * fa + stat_b[1:2] * fb
        acc = acc_a.astype(jnp.float32) * fa + acc_b.astype(jnp.float32) * fb
        return acc, jnp.concatenate([top, total], axis=0)

    def arrived(dirn, c, k):
        for copy in flights[dirn, c, k]:
            copy.wait_recv()
        return acc_recv[dirn, c, k], stat_recv[dirn, c, k]

    def mine(d, c):
        if d % side not in loaded:
            loaded.add(d % side)
            for copy in loads[d % side]:
                copy.wait()
        target = wrap(w + d, side)
        return accs[target, :, cols(c)], stats[target, :, cols(c)]

    for k in range(half):
        for c in (0, 1):
            for dirn in (0, 1):
                reach = far(dirn, c) - k
                if reach < 1:
                    continue
                acc, stat = mine((1, -1)[dirn] * reach, c)
                if k > 0:
                    acc, stat = merge((acc, stat), arrived(dirn, c, k - 1))
                acc_send[dirn, c, k] = acc.astype(jnp.bfloat16)
                stat_send[dirn, c, k] = stat
                launch(dirn, c, k, acc_send.at[dirn, c, k], stat_send.at[dirn, c, k])

    exchange = []
    for c in (0, 1):
        total = mine(0, c)
        for dirn in (1, 0):
            total = merge(total, arrived(dirn, c, far(dirn, c) - 1))
        acc, stat = total
        final = acc / stat[1:2]
        for j in range(part // tokens):
            block = jnp.transpose(final[:, j * tokens : (j + 1) * tokens])
            at = c * part // tokens + j
            result[:, at * HD : (at + 1) * HD] = block.astype(result.dtype)
    width = result.shape[1]
    spot = pl.ds(pl.multiple_of(me * width, width), width)
    for hop in range(1, peers):
        peer = lax.rem(me + hop, peers)
        copy = pltpu.make_async_remote_copy(
            src_ref=result.at[pl.ds(pl.multiple_of(peer * share, share), share)],
            dst_ref=out.at[:, spot],
            send_sem=xsend.at[hop],
            recv_sem=xrecv.at[hop],
            device_id={"heads": peer},
            device_id_type=MESH,
        )
        copy.start()
        exchange.append(copy)
    keep = pltpu.make_async_copy(
        result.at[pl.ds(pl.multiple_of(me * share, share), share)], out.at[:, spot], xlocal
    )
    keep.start()
    for copy in exchange:
        copy.wait_recv()
    for copy in exchange:
        copy.wait_send()
    keep.wait()
    for copies in flights.values():
        for copy in copies:
            copy.wait_send()


def return_partials(acc_all, stat_all, side, peers):
    half = side // 2
    rows = acc_all.shape[2]
    tokens = rows // GROUP
    part = rows // 2
    width = GROUP * HD
    anywhere = pl.BlockSpec(memory_space=pl.ANY)
    return pl.pallas_call(
        functools.partial(return_kernel, side),
        out_shape=jax.ShapeDtypeStruct((tokens // peers, peers * width), jnp.bfloat16),
        in_specs=[anywhere] * 2,
        out_specs=anywhere,
        scratch_shapes=[
            pltpu.VMEM(acc_all.shape, jnp.float32),
            pltpu.VMEM(stat_all.shape, jnp.float32),
            pltpu.VMEM((2, 2, half, HD, part), jnp.bfloat16),
            pltpu.VMEM((2, 2, half, 2, part), jnp.float32),
            pltpu.VMEM((2, 2, half, HD, part), jnp.bfloat16),
            pltpu.VMEM((2, 2, half, 2, part), jnp.float32),
            pltpu.VMEM((tokens, width), jnp.bfloat16),
            pltpu.SemaphoreType.DMA((2, 2, half, 2)),
            pltpu.SemaphoreType.DMA((2, 2, half, 2)),
            pltpu.SemaphoreType.DMA((side, 2)),
            pltpu.SemaphoreType.DMA((peers,)),
            pltpu.SemaphoreType.DMA((peers,)),
            pltpu.SemaphoreType.DMA,
        ],
        compiler_params=pltpu.CompilerParams(
            collective_id=1, has_side_effects=True, vmem_limit_bytes=48 << 20
        ),
        name="return_partials",
    )(acc_all, stat_all)


def per_device(
    queries,
    new_keys,
    new_values,
    library_keys,
    library_values,
    module_owner,
    module_page,
    module_count,
):
    rows_count = lax.axis_size("rows")
    peers = lax.axis_size("heads")
    side = math.isqrt(rows_count)
    pages = library_keys.shape[0]
    slots = module_owner.shape[1]
    live = jnp.arange(slots, dtype=jnp.int32)[None, :] < module_count[:, None]
    codes = jnp.where(live, module_owner * pages + module_page, -1)
    codes = jnp.pad(codes, ((0, 0), (0, 128 - slots)), constant_values=-1)
    k_all, v_all, q_all, t_all = gather_lines(library_keys, library_values, queries, codes, side)
    core, _, w = place(side)
    where = jnp.stack([core, w]).astype(jnp.int32)
    acc_all, stat_all = partials(t_all, where, q_all, new_keys, new_values, k_all, v_all, side)
    return return_partials(acc_all, stat_all, side, peers)


def solution(mesh):
    placed = (
        P("rows", "heads"),
        P("rows", "heads"),
        P("rows", "heads"),
        P("rows", None, "heads"),
        P("rows", None, "heads"),
        P("rows", None),
        P("rows", None),
        P("rows"),
    )
    return jax.shard_map(
        per_device,
        mesh=mesh,
        in_specs=placed,
        out_specs=P(("rows", "heads"), None),
        check_vma=False,
    )
```

time: 322 us -> 127 us (0.39)
  the two profiles are of different devices: /device:TPU:112 before, /device:TPU:1 now
where the time goes in v1:
time: 127 us; the launch traced here: 126 us
  Pallas kernels  117 us (92%)
  local copies, waits for them, and re-layouts  7.43 us (6%)
    pallas_call x1, Pallas kernels, gather_lines(): pl.pallas_call(functools.partial(gather_kernel, side), out_shape=shapes,...  64.7 us
    pallas_call x1, Pallas kernels, return_partials(): pl.pallas_call(functools.partial(return_kernel, side), out_shape=jax.Shap...  29.4 us
    pallas_call x1, Pallas kernels, partials(): pl.pallas_call(functools.partial(partial_kernel, side), grid=(side,), out...  23.3 us
    unnamed x13, local copies, waits for them, and re-layouts  7.42 us

profile of v1, /device:TPU:1, one launch (start us, length us, event | category | flops | bytes accessed | tf_op | source)
XLA Modules:
  0.0 126.3 jit_solution(4541722039962799420)
XLA Ops:
  0.7 0.1 pad_add_fusion.where_ref
  0.7 0.7 compare_select_fusion
  1.4 0.0 copy-start.1
  1.4 1.0 copy-done.1
  2.5 0.0 copy-start.2
  2.5 1.0 copy-done.2
  3.5 0.0 copy-start.3
  3.5 0.9 copy-done.3
  4.5 64.7 %gather_lines.1 = (bf16[8,16,128,128]{3,2,1,0:T(8,128)(2,1)}, bf16[8,16,128,128]{3,2,1,0:T(8,128)(2,1)}, bf16[8,128,1024]{2,1,0:T(8,128)(2,1)S(1)}, s32[8,1,128]{2,1,0:T(1,128)S(1)}) custom-call(bf16[16,128,128]{2,1,0:T(8,128)(2,1)S(1)} %copy-done.1, bf16[16,128,128]{2,1,0:T(8,128)(2,1)S(1)} %copy-done.2, bf16[128,1024]{1,0:T(8,128)(2,1)S(1)} %copy-done.3, ...), custom_call_target="tpu_custom_call" | custom-call | tf_op jit(solution)/shard_map/gather_lines/pallas_call | solution.py:116
  69.1 0.0 copy-start.4
  69.2 0.7 copy-done.4
  69.9 0.0 copy-start.5
  69.9 0.8 copy-done.5
  70.7 23.3 %partials.1 = (f32[8,128,1024]{2,1,0:T(8,128)}, f32[8,2,1024]{2,1,0:T(2,128)S(1)}) custom-call(s32[8,1,128]{2,1,0:T(1,128)S(1)} %get-tuple-element.11.codes, s32[2]{0:T(128)S(1)} %pad_add_fusion.where_ref, bf16[8,128,1024]{2,1,0:T(8,128)(2,1)S(1)} %get-tuple-element.12.q_ref, bf16[128,128]{1,0:T(8,128)(2,1)S(1)} %copy-done.4, ...), custom_call_target="tpu_custom_call" | custom-call | tf_op jit(solution)/shard_map/partials/pallas_call | solution.py:243
  94.0 0.0 copy-start
  94.0 2.2 %copy-done = f32[8,128,1024]{2,1,0:T(8,128)S(1)} copy-done((f32[8,128,1024]{2,1,0:T(8,128)S(1)}, f32[8,128,1024]{2,1,0:T(8,128)}, u32[]{:S(2)}) %copy-start) | copy-done | bytes 4194328
  96.2 29.4 %return_partials.1 = bf16[16,8192]{1,0:T(8,128)(2,1)S(1)} custom-call(f32[8,128,1024]{2,1,0:T(8,128)S(1)} %copy-done, f32[8,2,1024]{2,1,0:T(2,128)S(1)} %get-tuple-element.16.stat_hbm), custom_call_target="tpu_custom_call" | custom-call | tf_op jit(solution)/shard_map/return_partials/pallas_call | solution.py:415
  125.6 0.7 copy.11
  (1 shorter events, 0.0 us)
Async XLA Ops:
  1.4 1.0 copy-start.1
  2.5 1.0 copy-start.2
  3.5 0.9 copy-start.3
  69.1 0.8 copy-start.4
  69.9 0.8 copy-start.5
  94.0 2.2 %copy-start = (f32[8,128,1024]{2,1,0:T(8,128)S(1)}, f32[8,128,1024]{2,1,0:T(8,128)}, u32[]{:S(2)}) copy-start(f32[8,128,1024]{2,1,0:T(8,128)} %get-tuple-element.15.acc_hbm) | copy-start | bytes 12582916

commit v2 on v1

v2 whole, which is shorter than its diff:
```python
import functools
import math

import jax
import jax.numpy as jnp
from jax import lax
from jax.experimental import pallas as pl
from jax.experimental.pallas import tpu as pltpu
from jax.sharding import PartitionSpec as P

HD = 128
QH = 64
KVH = 8
GROUP = QH // KVH
MESH = pl.DeviceIdType.MESH
LOG2E = 1.4426950408889634
FLOOR = -1e30


def place(side):
    row = lax.axis_index("rows")
    core = lax.rem(lax.axis_index("heads"), 2)
    z, y = row // side, lax.rem(row, side)
    u = (1 - core) * z + core * y
    w = (1 - core) * y + core * z
    return core, u, w


def row_of(core, u, w, side):
    return (1 - core) * (u * side + w) + core * (w * side + u)


def wrap(value, side):
    return lax.rem(value + 4 * side, side)


def gather_kernel(
    side, owner, page, count, k_in, v_in, q_in, k_all, v_all, q_all, t_all, vraw, qraw, vt, qt, table, send, recv, local
):
    core, u, w = place(side)
    half = side // 2
    heads_wide = qt.shape[1] // 2
    slots = owner.shape[1]
    pages = k_in.shape[0]
    tokens = qraw.shape[0]
    lib_at = [row_of(core, wrap(u + d, side), w, side) for d in (1, -1)]
    que_at = [row_of(core, u, wrap(w + d, side), side) for d in (1, -1)]

    barrier = pltpu.get_barrier_semaphore()
    for row in lib_at + que_at:
        pl.semaphore_signal(barrier, inc=1, device_id={"rows": row}, device_id_type=MESH)
    fetch_q = pltpu.make_async_copy(q_in, qraw, local.at[4])
    fetch_v = pltpu.make_async_copy(v_in, vraw, local.at[5])
    fetch_q.start()
    fetch_v.start()
    own = [pltpu.make_async_copy(k_in, k_all.at[u], local.at[0])]
    own[0].start()

    line_at = lax.broadcasted_iota(jnp.int32, table.shape, 0)
    lane_at = lax.broadcasted_iota(jnp.int32, table.shape, 1)
    filled = jnp.zeros(table.shape, jnp.int32)
    packed = jnp.zeros(table.shape, jnp.int32)
    for slot in range(slots):
        z, y = owner[0, slot] // side, lax.rem(owner[0, slot], side)
        line = (1 - core) * z + core * y
        cross = (1 - core) * y + core * z
        hit = jnp.logical_and(line_at == cross, count[0] > slot)
        packed = jnp.where(jnp.logical_and(hit, lane_at == filled), line * pages + page[0, slot], packed)
        filled = filled + jnp.where(hit, 1, 0)
    table[...] = jnp.where(lane_at == table.shape[1] - 1, filled, packed)

    started = {}
    waited = set()

    def start(dirn, step, kind):
        sign = (1, -1)[dirn]
        u0, w0 = wrap(u - sign * step, side), wrap(w - sign * step, side)
        if step > 0:
            started[dirn, step - 1, kind].wait_recv()
            waited.add((dirn, step - 1, kind))
        own_ref, all_ref, row = (
            (k_in, k_all.at[u0], lib_at[dirn]),
            (vt, v_all.at[u0], lib_at[dirn]),
            (qt, q_all.at[w0], que_at[dirn]),
            (table, t_all.at[w0], que_at[dirn]),
        )[kind]
        src, dst = (own_ref if step == 0 else all_ref), all_ref
        if kind == 2 and step == half - 1:
            cols = pl.ds(dirn * heads_wide, heads_wide)
            src, dst = all_ref.at[:, cols], all_ref.at[:, cols]
        copy = pltpu.make_async_remote_copy(
            src_ref=src,
            dst_ref=dst,
            send_sem=send.at[dirn, step, kind],
            recv_sem=recv.at[dirn, step, kind],
            device_id={"rows": row},
            device_id_type=MESH,
        )
        copy.start()
        started[dirn, step, kind] = copy

    def keep(src, dst, kind):
        copy = pltpu.make_async_copy(src, dst, local.at[kind])
        copy.start()
        own.append(copy)

    pl.semaphore_wait(barrier, 4)
    for dirn in (0, 1):
        start(dirn, 0, 3)
        start(dirn, 0, 0)
    fetch_q.wait()
    for j in range(GROUP):
        qt[:, j * tokens : (j + 1) * tokens] = jnp.transpose(qraw[:, j * HD : (j + 1) * HD])
    for dirn in (0, 1):
        start(dirn, 0, 2)
    fetch_v.wait()
    for j in range(pages):
        vt[j] = jnp.transpose(vraw[j])
    for dirn in (0, 1):
        start(dirn, 0, 1)
    keep(vt, v_all.at[u], 1)
    keep(qt, q_all.at[w], 2)
    keep(table, t_all.at[w], 3)
    for step in range(1, half):
        last = step == half - 1
        for kind in (3, 0, 2, 1):
            for dirn in (0, 1):
                if last and (dirn, kind) in ((1, 0), (0, 1), (1, 3)):
                    continue
                start(dirn, step, kind)
    for key, copy in started.items():
        if key not in waited:
            copy.wait_recv()
    for copy in started.values():
        copy.wait_send()
    for copy in own:
        copy.wait()


HBM = pl.BlockSpec(memory_space=pltpu.HBM)
SMEM = pl.BlockSpec(memory_space=pltpu.SMEM)
VMEM = pl.BlockSpec(memory_space=pltpu.VMEM)


def gather_lines(owner, page, count, k, v, q, side):
    half = side // 2
    tokens = q.shape[0]
    qt = (HD, GROUP * tokens)
    table = (side, 128)
    return pl.pallas_call(
        functools.partial(gather_kernel, side),
        out_shape=[
            jax.ShapeDtypeStruct((side,) + k.shape, k.dtype),
            jax.ShapeDtypeStruct((side,) + v.shape, v.dtype),
            jax.ShapeDtypeStruct((side,) + qt, q.dtype),
            jax.ShapeDtypeStruct((side,) + table, jnp.int32),
        ],
        in_specs=[SMEM] * 3 + [HBM] * 3,
        out_specs=[HBM] * 4,
        scratch_shapes=[
            pltpu.VMEM(v.shape, v.dtype),
            pltpu.VMEM(q.shape, q.dtype),
            pltpu.VMEM(v.shape, v.dtype),
            pltpu.VMEM(qt, q.dtype),
            pltpu.VMEM(table, jnp.int32),
            pltpu.SemaphoreType.DMA((2, half, 4)),
            pltpu.SemaphoreType.DMA((2, half, 4)),
            pltpu.SemaphoreType.DMA((6,)),
        ],
        compiler_params=pltpu.CompilerParams(
            collective_id=0, has_side_effects=True
        ),
        name="gather_lines",
    )(owner, page, count, k, v, q)


def partial_kernel(
    side, table, nk_ref, nv_ref, q_hbm, k_hbm, v_hbm, acc_out, stat_out, qbuf, kbuf, vbuf, acc, stat, qsem, ksem, vsem, osem
):
    _, _, w = place(side)
    slots = kbuf.shape[0] // side
    pages = k_hbm.shape[1]
    scale = LOG2E / math.sqrt(HD)
    rows = qbuf.shape[2]
    tokens = nk_ref.shape[0]
    wide = 2 * tokens
    chunks = [slice(c * wide, (c + 1) * wide) for c in range(rows // wide)]

    def listed(req):
        return table[req, w, table.shape[2] - 1]

    def page_copies(turn, k, value):
        at = turn * slots + k
        line, page = value // pages, lax.rem(value, pages)
        return (
            pltpu.make_async_copy(k_hbm.at[line, page], kbuf.at[at], ksem.at[at]),
            pltpu.make_async_copy(v_hbm.at[line, page], vbuf.at[at], vsem.at[at]),
        )

    def q_copy(turn):
        return pltpu.make_async_copy(q_hbm.at[wrap(w + turn, side)], qbuf.at[turn], qsem.at[turn])

    def out_copies(turn):
        spot, req = lax.rem(turn, 2), wrap(w + turn, side)
        return (
            pltpu.make_async_copy(acc.at[spot], acc_out.at[req], osem.at[spot, 0]),
            pltpu.make_async_copy(stat.at[spot], stat_out.at[req], osem.at[spot, 1]),
        )

    @pl.loop(0, side)
    def _(turn):
        q_copy(turn).start()
        req = wrap(w + turn, side)

        @pl.loop(0, listed(req))
        def _(k):
            for copy in page_copies(turn, k, table[req, w, k]):
                copy.start()

    def dot(one, two):
        return jnp.dot(one, two, preferred_element_type=jnp.float32)

    @pl.loop(0, side)
    def _(turn):
        spot, req = lax.rem(turn, 2), wrap(w + turn, side)

        @pl.when(turn >= 2)
        def _():
            for copy in out_copies(turn - 2):
                copy.wait()

        q_copy(turn).wait()

        @pl.when(turn > 0)
        def _():
            acc[spot] = jnp.zeros((HD, rows), jnp.float32)
            stat[spot, 0:1] = jnp.full((1, rows), FLOOR, jnp.float32)
            stat[spot, 1:2] = jnp.zeros((1, rows), jnp.float32)

        @pl.when(turn == 0)
        def _():
            keys, values = nk_ref[...], jnp.transpose(nv_ref[...])
            for cols in chunks:
                raw = dot(keys, qbuf[turn, :, cols])
                key_at = lax.broadcasted_iota(jnp.int32, raw.shape, 0)
                token_at = lax.rem(lax.broadcasted_iota(jnp.int32, raw.shape, 1), tokens)
                allowed = key_at <= token_at
                raw = jnp.where(allowed, raw, FLOOR)
                top = jnp.max(raw, axis=0, keepdims=True) * scale
                weights = jnp.where(allowed, jnp.exp2(raw * scale - top), 0.0)
                stat[spot, 0:1, cols] = top
                stat[spot, 1:2, cols] = jnp.sum(weights, axis=0, keepdims=True)
                acc[spot, :, cols] = dot(values, weights.astype(jnp.bfloat16))

        @pl.loop(0, listed(req))
        def _(k):
            for copy in page_copies(turn, k, table[req, w, k]):
                copy.wait()
            at = turn * slots + k
            keys, values = kbuf[at], vbuf[at]
            for cols in chunks:
                raw = dot(keys, qbuf[turn, :, cols])
                old = stat[spot, 0:1, cols]
                top = jnp.maximum(old, jnp.max(raw, axis=0, keepdims=True) * scale)
                weights = jnp.exp2(raw * scale - top)
                shrink = jnp.exp2(old - top)
                stat[spot, 0:1, cols] = top
                stat[spot, 1:2, cols] = stat[spot, 1:2, cols] * shrink + jnp.sum(weights, axis=0, keepdims=True)
                acc[spot, :, cols] = acc[spot, :, cols] * shrink + dot(values, weights.astype(jnp.bfloat16))

        for copy in out_copies(turn):
            copy.start()

    for turn in (side - 2, side - 1):
        for copy in out_copies(turn):
            copy.wait()


def partials(table, q_all, nk, nv, k_all, v_all, slots, side):
    rows = q_all.shape[2]
    page = k_all.shape[2:]
    return pl.pallas_call(
        functools.partial(partial_kernel, side),
        out_shape=[
            jax.ShapeDtypeStruct((side, HD, rows), jnp.float32),
            jax.ShapeDtypeStruct((side, 2, rows), jnp.float32),
        ],
        in_specs=[SMEM, VMEM, VMEM, HBM, HBM, HBM],
        out_specs=[HBM, HBM],
        scratch_shapes=[
            pltpu.VMEM(q_all.shape, jnp.bfloat16),
            pltpu.VMEM((side * slots,) + page, jnp.bfloat16),
            pltpu.VMEM((side * slots,) + page, jnp.bfloat16),
            pltpu.VMEM((2, HD, rows), jnp.float32),
            pltpu.VMEM((2, 2, rows), jnp.float32),
            pltpu.SemaphoreType.DMA((side,)),
            pltpu.SemaphoreType.DMA((side * slots,)),
            pltpu.SemaphoreType.DMA((side * slots,)),
            pltpu.SemaphoreType.DMA((2, 2)),
        ],
        name="partials",
    )(table, nk, nv, q_all, k_all, v_all)


def return_kernel(
    side, acc_hbm, stat_hbm, out, accs, stats, acc_send, stat_send, acc_recv, stat_recv, result, send, recv, load, xsend, xrecv, xlocal
):
    core, u, w = place(side)
    me = lax.axis_index("heads")
    peers = lax.axis_size("heads")
    half = side // 2
    rows = accs.shape[2]
    part = rows // 2
    tokens = result.shape[0]
    share = tokens // peers
    near = [row_of(core, u, wrap(w + d, side), side) for d in (1, -1)]

    barrier = pltpu.get_barrier_semaphore()
    for row in near:
        pl.semaphore_signal(barrier, inc=1, device_id={"rows": row}, device_id_type=MESH)
    for hop in range(1, peers):
        pl.semaphore_signal(
            barrier, inc=1, device_id={"heads": lax.rem(me + hop, peers)}, device_id_type=MESH
        )
    order = [half, half - 1, half + 1] + [d for k in range(half - 2, 0, -1) for d in (k, side - k)] + [0]
    loads = {}
    for d in order:
        target = wrap(w + d, side)
        loads[d] = [
            pltpu.make_async_copy(acc_hbm.at[target], accs.at[target], load.at[d, 0]),
            pltpu.make_async_copy(stat_hbm.at[target], stats.at[target], load.at[d, 1]),
        ]
        for copy in loads[d]:
            copy.start()
    loaded = set()
    pl.semaphore_wait(barrier, 1 + peers)

    def cols(c):
        return slice(c * part, (c + 1) * part)

    def far(dirn, c):
        return half if dirn == c else half - 1

    flights = {}

    def launch(dirn, c, k, acc_src, stat_src):
        copies = [
            pltpu.make_async_remote_copy(
                src_ref=src,
                dst_ref=dst,
                send_sem=send.at[dirn, c, k, kind],
                recv_sem=recv.at[dirn, c, k, kind],
                device_id={"rows": near[dirn]},
                device_id_type=MESH,
            )
            for kind, (src, dst) in enumerate(
                [(stat_src, stat_recv.at[dirn, c, k]), (acc_src, acc_recv.at[dirn, c, k])]
            )
        ]
        for copy in copies:
            copy.start()
        flights[dirn, c, k] = copies

    def merge(one, two):
        (acc_a, stat_a), (acc_b, stat_b) = one, two
        top = jnp.maximum(stat_a[0:1], stat_b[0:1])
        fa, fb = jnp.exp2(stat_a[0:1] - top), jnp.exp2(stat_b[0:1] - top)
        total = stat_a[1:2] * fa + stat_b[1:2] * fb
        acc = acc_a.astype(jnp.float32) * fa + acc_b.astype(jnp.float32) * fb
        return acc, jnp.concatenate([top, total], axis=0)

    def arrived(dirn, c, k):
        for copy in flights[dirn, c, k]:
            copy.wait_recv()
        return acc_recv[dirn, c, k], stat_recv[dirn, c, k]

    def mine(d, c):
        if d % side not in loaded:
            loaded.add(d % side)
            for copy in loads[d % side]:
                copy.wait()
        target = wrap(w + d, side)
        return accs[target, :, cols(c)], stats[target, :, cols(c)]

    for k in range(half):
        for c in (0, 1):
            for dirn in (0, 1):
                reach = far(dirn, c) - k
                if reach < 1:
                    continue
                acc, stat = mine((1, -1)[dirn] * reach, c)
                if k > 0:
                    acc, stat = merge((acc, stat), arrived(dirn, c, k - 1))
                acc_send[dirn, c, k] = acc.astype(jnp.bfloat16)
                stat_send[dirn, c, k] = stat
                launch(dirn, c, k, acc_send.at[dirn, c, k], stat_send.at[dirn, c, k])

    exchange = []
    for c in (0, 1):
        total = mine(0, c)
        for dirn in (1, 0):
            total = merge(total, arrived(dirn, c, far(dirn, c) - 1))
        acc, stat = total
        final = acc / stat[1:2]
        for j in range(part // tokens):
            block = jnp.transpose(final[:, j * tokens : (j + 1) * tokens])
            at = c * part // tokens + j
            result[:, at * HD : (at + 1) * HD] = block.astype(result.dtype)
    width = result.shape[1]
    spot = pl.ds(pl.multiple_of(me * width, width), width)
    for hop in range(1, peers):
        peer = lax.rem(me + hop, peers)
        copy = pltpu.make_async_remote_copy(
            src_ref=result.at[pl.ds(pl.multiple_of(peer * share, share), share)],
            dst_ref=out.at[:, spot],
            send_sem=xsend.at[hop],
            recv_sem=xrecv.at[hop],
            device_id={"heads": peer},
            device_id_type=MESH,
        )
        copy.start()
        exchange.append(copy)
    keep = pltpu.make_async_copy(
        result.at[pl.ds(pl.multiple_of(me * share, share), share)], out.at[:, spot], xlocal
    )
    keep.start()
    for copy in exchange:
        copy.wait_recv()
    for copy in exchange:
        copy.wait_send()
    keep.wait()
    for copies in flights.values():
        for copy in copies:
            copy.wait_send()


def return_partials(acc_all, stat_all, side, peers):
    half = side // 2
    rows = acc_all.shape[2]
    tokens = rows // GROUP
    part = rows // 2
    width = GROUP * HD
    return pl.pallas_call(
        functools.partial(return_kernel, side),
        out_shape=jax.ShapeDtypeStruct((tokens // peers, peers * width), jnp.bfloat16),
        in_specs=[HBM] * 2,
        out_specs=HBM,
        scratch_shapes=[
            pltpu.VMEM(acc_all.shape, jnp.float32),
            pltpu.VMEM(stat_all.shape, jnp.float32),
            pltpu.VMEM((2, 2, half, HD, part), jnp.bfloat16),
            pltpu.VMEM((2, 2, half, 2, part), jnp.float32),
            pltpu.VMEM((2, 2, half, HD, part), jnp.bfloat16),
            pltpu.VMEM((2, 2, half, 2, part), jnp.float32),
            pltpu.VMEM((tokens, width), jnp.bfloat16),
            pltpu.SemaphoreType.DMA((2, 2, half, 2)),
            pltpu.SemaphoreType.DMA((2, 2, half, 2)),
            pltpu.SemaphoreType.DMA((side, 2)),
            pltpu.SemaphoreType.DMA((peers,)),
            pltpu.SemaphoreType.DMA((peers,)),
            pltpu.SemaphoreType.DMA,
        ],
        compiler_params=pltpu.CompilerParams(
            collective_id=1, has_side_effects=True
        ),
        name="return_partials",
    )(acc_all, stat_all)


def per_device(
    queries,
    new_keys,
    new_values,
    library_keys,
    library_values,
    module_owner,
    module_page,
    module_count,
):
    rows_count = lax.axis_size("rows")
    peers = lax.axis_size("heads")
    side = math.isqrt(rows_count)
    slots = module_owner.shape[1]
    k_all, v_all, q_all, table = gather_lines(
        module_owner, module_page, module_count, library_keys, library_values, queries, side
    )
    acc_all, stat_all = partials(table, q_all, new_keys, new_values, k_all, v_all, slots, side)
    return return_partials(acc_all, stat_all, side, peers)


def solution(mesh):
    placed = (
        P("rows", "heads"),
        P("rows", "heads"),
        P("rows", "heads"),
        P("rows", None, "heads"),
        P("rows", None, "heads"),
        P("rows", None),
        P("rows", None),
        P("rows"),
    )
    return jax.shard_map(
        per_device,
        mesh=mesh,
        in_specs=placed,
        out_specs=P(("rows", "heads"), None),
        check_vma=False,
    )
```

time: 127 us -> 112 us (0.88)
  Pallas kernels: 117 us -> 110 us
  local copies, waits for them, and re-layouts: 7.43 us -> 1.67 us
    pallas_call x2, Pallas kernels: 88 us -> 80.7 us  [the longest x1 66.4 us: gather_lines(): pl.pallas_call(functools.partial(gather_kernel, side), out_shape=[jax.Sha...]
    unnamed x13 -> x1, local copies, waits for them, and re-layouts: 7.42 us -> 1.67 us
where the time goes in v2:
time: 112 us
  Pallas kernels  110 us (98%)
  local copies, waits for them, and re-layouts  1.67 us (1%)
    pallas_call x1, Pallas kernels, gather_lines(): pl.pallas_call(functools.partial(gather_kernel, side), out_shape=[jax.Sha...  66.4 us
    pallas_call x1, Pallas kernels, return_partials(): pl.pallas_call(functools.partial(return_kernel, side), out_shape=jax.Shap...  28.9 us
    pallas_call x1, Pallas kernels, partials(): pl.pallas_call(functools.partial(partial_kernel, side), out_shape=[jax.Sh...  14.3 us

profile of v2, /device:TPU:1, one launch (start us, length us, event | category | flops | bytes accessed | tf_op | source)
XLA Modules:
  0.0 112.0 jit_solution(5919050595818063432)
XLA Ops:
  0.7 66.4 %gather_lines.1 = (bf16[8,16,128,128]{3,2,1,0:T(8,128)(2,1)}, bf16[8,16,128,128]{3,2,1,0:T(8,128)(2,1)}, bf16[8,128,1024]{2,1,0:T(8,128)(2,1)}, s32[8,8,128]{2,1,0:T(8,128)}) custom-call(s32[1,16]{1,0:T(1,128)} %owner.1, s32[1,16]{1,0:T(1,128)} %page.1, s32[1]{0:T(128)S(6)} %copy.10.count, bf16[16,128,128]{2,1,0:T(8,128)(2,1)} %k_in.1, ...), custom_call_target="tpu_custom_call" | custom-call | tf_op jit(solution)/shard_map/gather_lines/pallas_call | solution.py:150
  67.1 14.3 %partials.1 = (f32[8,128,1024]{2,1,0:T(8,128)}, f32[8,2,1024]{2,1,0:T(2,128)}) custom-call(s32[8,8,128]{2,1,0:T(8,128)} %get-tuple-element.11.table, bf16[128,128]{1,0:T(8,128)(2,1)} %nk_ref.1, bf16[128,128]{1,0:T(8,128)(2,1)} %nv_ref.1, bf16[8,128,1024]{2,1,0:T(8,128)(2,1)} %get-tuple-element.12.q_hbm, bf16[8,16,128,128]{3,2,1,0:T(8,128)(2,1)} %get-tuple-element.13.k_hbm, ...), custom_call_target="tpu_custom_call" | custom-call | tf_op jit(solution)/shard_map/partials/pallas_call | solution.py:282
  81.4 28.9 %return_partials.1 = bf16[16,8192]{1,0:T(8,128)(2,1)} custom-call(f32[8,128,1024]{2,1,0:T(8,128)} %get-tuple-element.15.acc_hbm, f32[8,2,1024]{2,1,0:T(2,128)} %get-tuple-element.16.stat_hbm), custom_call_target="tpu_custom_call" | custom-call | tf_op jit(solution)/shard_map/return_partials/pallas_call | solution.py:443
  110.3 1.7 %copy.11 = bf16[16,8192]{1,0:T(8,128)(2,1)} copy(bf16[16,8192]{1,0:T(8,128)(2,1)} %return_partials.1) | data formatting | bytes 524288

commit v3 on v2

v3 whole, which is shorter than its diff:
```python
import functools
import math

import jax
import jax.numpy as jnp
from jax import lax
from jax.experimental import pallas as pl
from jax.experimental.pallas import tpu as pltpu
from jax.sharding import PartitionSpec as P

HD = 128
QH = 64
KVH = 8
GROUP = QH // KVH
MESH = pl.DeviceIdType.MESH
LOG2E = 1.4426950408889634
FLOOR = -1e30


def place(side):
    row = lax.axis_index("rows")
    core = lax.rem(lax.axis_index("heads"), 2)
    z, y = row // side, lax.rem(row, side)
    u = (1 - core) * z + core * y
    w = (1 - core) * y + core * z
    return core, u, w


def row_of(core, u, w, side):
    return (1 - core) * (u * side + w) + core * (w * side + u)


def wrap(value, side):
    return lax.rem(value + 4 * side, side)


def gather_kernel(
    side, owner_in, page_in, count, k_in, v_in, q_in, k_all, v_all, q_all, t_all, owner, page, vraw, qraw, send, recv, local
):
    core, u, w = place(side)
    half = side // 2
    heads_wide = q_all.shape[2] // 2
    shape = t_all.shape[1:]
    slots = owner.shape[1]
    pages = k_in.shape[0]
    tokens = qraw.shape[0]
    lib_at = [row_of(core, wrap(u + d, side), w, side) for d in (1, -1)]
    que_at = [row_of(core, u, wrap(w + d, side), side) for d in (1, -1)]

    barrier = pltpu.get_barrier_semaphore()
    for row in lib_at + que_at:
        pl.semaphore_signal(barrier, inc=1, device_id={"rows": row}, device_id_type=MESH)
    fetch_q = pltpu.make_async_copy(q_in, qraw, local.at[4])
    fetch_v = pltpu.make_async_copy(v_in, vraw, local.at[5])
    lists = [
        pltpu.make_async_copy(owner_in, owner, local.at[1]),
        pltpu.make_async_copy(page_in, page, local.at[2]),
    ]
    for copy in lists:
        copy.start()
    fetch_q.start()
    fetch_v.start()
    own = [pltpu.make_async_copy(k_in, k_all.at[u], local.at[0])]
    own[0].start()

    pl.semaphore_wait(barrier, 4)
    started = {}
    waited = set()

    def start(dirn, step, kind):
        sign = (1, -1)[dirn]
        u0, w0 = wrap(u - sign * step, side), wrap(w - sign * step, side)
        if step > 0:
            started[dirn, step - 1, kind].wait_recv()
            waited.add((dirn, step - 1, kind))
        all_ref, row = (
            (k_all.at[u0], lib_at[dirn]),
            (v_all.at[u0], lib_at[dirn]),
            (q_all.at[w0], que_at[dirn]),
            (t_all.at[w0], que_at[dirn]),
        )[kind]
        src, dst = (k_in if step == 0 and kind == 0 else all_ref), all_ref
        if kind == 2 and step == half - 1:
            cols = pl.ds(dirn * heads_wide, heads_wide)
            src, dst = all_ref.at[:, cols], all_ref.at[:, cols]
        copy = pltpu.make_async_remote_copy(
            src_ref=src,
            dst_ref=dst,
            send_sem=send.at[dirn, step, kind],
            recv_sem=recv.at[dirn, step, kind],
            device_id={"rows": row},
            device_id_type=MESH,
        )
        copy.start()
        started[dirn, step, kind] = copy

    for dirn in (0, 1):
        start(dirn, 0, 0)
    for copy in lists:
        copy.wait()
    line_at = lax.broadcasted_iota(jnp.int32, shape, 0)
    lane_at = lax.broadcasted_iota(jnp.int32, shape, 1)
    filled = jnp.zeros(shape, jnp.int32)
    packed = jnp.zeros(shape, jnp.int32)
    for slot in range(slots):
        z, y = owner[0, slot] // side, lax.rem(owner[0, slot], side)
        line = (1 - core) * z + core * y
        cross = (1 - core) * y + core * z
        hit = jnp.logical_and(line_at == cross, count[0] > slot)
        packed = jnp.where(jnp.logical_and(hit, lane_at == filled), line * pages + page[0, slot], packed)
        filled = filled + jnp.where(hit, 1, 0)
    t_all[w] = jnp.where(lane_at == shape[1] - 1, filled, packed)
    for dirn in (0, 1):
        start(dirn, 0, 3)
    fetch_q.wait()
    for j in range(GROUP):
        q_all[w, :, j * tokens : (j + 1) * tokens] = jnp.transpose(qraw[:, j * HD : (j + 1) * HD])
    for dirn in (0, 1):
        start(dirn, 0, 2)
    fetch_v.wait()
    for j in range(pages):
        v_all[u, j] = jnp.transpose(vraw[j])
    for dirn in (0, 1):
        start(dirn, 0, 1)
    for step in range(1, half):
        last = step == half - 1
        for kind in (3, 0, 2, 1):
            for dirn in (0, 1):
                if last and (dirn, kind) in ((1, 0), (0, 1), (1, 3)):
                    continue
                start(dirn, step, kind)
    for key, copy in started.items():
        if key not in waited:
            copy.wait_recv()
    for copy in started.values():
        copy.wait_send()
    for copy in own:
        copy.wait()


HBM = pl.BlockSpec(memory_space=pltpu.HBM)
SMEM = pl.BlockSpec(memory_space=pltpu.SMEM)
VMEM = pl.BlockSpec(memory_space=pltpu.VMEM)


def in_hbm(a):
    return pltpu.with_memory_space_constraint(a, pltpu.HBM)


def gather_lines(owner, page, count, k, v, q, side):
    half = side // 2
    tokens = q.shape[0]
    return pl.pallas_call(
        functools.partial(gather_kernel, side),
        out_shape=[
            pltpu.VMEM((side,) + k.shape, k.dtype),
            pltpu.VMEM((side,) + v.shape, v.dtype),
            pltpu.VMEM((side, HD, GROUP * tokens), q.dtype),
            pltpu.VMEM((side, side, 128), jnp.int32),
        ],
        in_specs=[HBM, HBM, SMEM, HBM, HBM, HBM],
        out_specs=[VMEM] * 4,
        scratch_shapes=[
            pltpu.SMEM(owner.shape, owner.dtype),
            pltpu.SMEM(page.shape, page.dtype),
            pltpu.VMEM(v.shape, v.dtype),
            pltpu.VMEM(q.shape, q.dtype),
            pltpu.SemaphoreType.DMA((2, half, 4)),
            pltpu.SemaphoreType.DMA((2, half, 4)),
            pltpu.SemaphoreType.DMA((6,)),
        ],
        compiler_params=pltpu.CompilerParams(
            collective_id=0, has_side_effects=True, vmem_limit_bytes=16 << 20
        ),
        name="gather_lines",
    )(in_hbm(owner), in_hbm(page), count, in_hbm(k), in_hbm(v), in_hbm(q))


def partial_kernel(side, table, nk_hbm, nv_hbm, q_all, k_all, v_all, acc, stat, nk, nv, fetched):
    _, _, w = place(side)
    pages = k_all.shape[1]
    scale = LOG2E / math.sqrt(HD)
    rows = q_all.shape[2]
    tokens = nk.shape[0]
    wide = 2 * tokens
    chunks = [slice(c * wide, (c + 1) * wide) for c in range(rows // wide)]
    fetches = [
        pltpu.make_async_copy(nk_hbm, nk, fetched.at[0]),
        pltpu.make_async_copy(nv_hbm, nv, fetched.at[1]),
    ]
    for copy in fetches:
        copy.start()

    def dot(one, two):
        return jnp.dot(one, two, preferred_element_type=jnp.float32)

    def add(req, keys, values, causal):
        for cols in chunks:
            raw = dot(keys, q_all[req, :, cols])
            if causal:
                key_at = lax.broadcasted_iota(jnp.int32, raw.shape, 0)
                token_at = lax.rem(lax.broadcasted_iota(jnp.int32, raw.shape, 1), tokens)
                allowed = key_at <= token_at
                raw = jnp.where(allowed, raw, FLOOR)
            old = stat[req, 0:1, cols]
            top = jnp.maximum(old, jnp.max(raw, axis=0, keepdims=True) * scale)
            weights = jnp.exp2(raw * scale - top)
            if causal:
                weights = jnp.where(allowed, weights, 0.0)
            shrink = jnp.exp2(old - top)
            stat[req, 0:1, cols] = top
            stat[req, 1:2, cols] = stat[req, 1:2, cols] * shrink + jnp.sum(weights, axis=0, keepdims=True)
            acc[req, :, cols] = acc[req, :, cols] * shrink + dot(values, weights.astype(jnp.bfloat16))

    @pl.loop(0, side)
    def _(req):
        acc[req] = jnp.zeros((HD, rows), jnp.float32)
        stat[req, 0:1] = jnp.full((1, rows), FLOOR, jnp.float32)
        stat[req, 1:2] = jnp.zeros((1, rows), jnp.float32)

        @pl.loop(0, table[req, w, table.shape[2] - 1])
        def _(k):
            value = table[req, w, k]
            line, page = value // pages, lax.rem(value, pages)
            add(req, k_all[line, page], v_all[line, page], False)

    for copy in fetches:
        copy.wait()
    add(w, nk[...], jnp.transpose(nv[...]), True)


def partials(table, q_all, nk, nv, k_all, v_all, side):
    rows = q_all.shape[2]
    return pl.pallas_call(
        functools.partial(partial_kernel, side),
        out_shape=[
            pltpu.VMEM((side, HD, rows), jnp.float32),
            pltpu.VMEM((side, 2, rows), jnp.float32),
        ],
        in_specs=[SMEM, HBM, HBM, VMEM, VMEM, VMEM],
        out_specs=[VMEM, VMEM],
        scratch_shapes=[
            pltpu.VMEM(nk.shape, nk.dtype),
            pltpu.VMEM(nv.shape, nv.dtype),
            pltpu.SemaphoreType.DMA((2,)),
        ],
        compiler_params=pltpu.CompilerParams(vmem_limit_bytes=16 << 20),
        name="partials",
    )(table, in_hbm(nk), in_hbm(nv), q_all, k_all, v_all)


def return_kernel(
    side, accs, stats, out, acc_send, stat_send, acc_recv, stat_recv, result, send, recv, xsend, xrecv, xlocal
):
    core, u, w = place(side)
    me = lax.axis_index("heads")
    peers = lax.axis_size("heads")
    half = side // 2
    rows = accs.shape[2]
    part = rows // 2
    tokens = result.shape[0]
    share = tokens // peers
    near = [row_of(core, u, wrap(w + d, side), side) for d in (1, -1)]

    barrier = pltpu.get_barrier_semaphore()
    for row in near:
        pl.semaphore_signal(barrier, inc=1, device_id={"rows": row}, device_id_type=MESH)
    for hop in range(1, peers):
        pl.semaphore_signal(
            barrier, inc=1, device_id={"heads": lax.rem(me + hop, peers)}, device_id_type=MESH
        )
    pl.semaphore_wait(barrier, 1 + peers)

    def cols(c):
        return slice(c * part, (c + 1) * part)

    def far(dirn, c):
        return half if dirn == c else half - 1

    flights = {}

    def launch(dirn, c, k, acc_src, stat_src):
        copies = [
            pltpu.make_async_remote_copy(
                src_ref=src,
                dst_ref=dst,
                send_sem=send.at[dirn, c, k, kind],
                recv_sem=recv.at[dirn, c, k, kind],
                device_id={"rows": near[dirn]},
                device_id_type=MESH,
            )
            for kind, (src, dst) in enumerate(
                [(stat_src, stat_recv.at[dirn, c, k]), (acc_src, acc_recv.at[dirn, c, k])]
            )
        ]
        for copy in copies:
            copy.start()
        flights[dirn, c, k] = copies

    def merge(one, two):
        (acc_a, stat_a), (acc_b, stat_b) = one, two
        top = jnp.maximum(stat_a[0:1], stat_b[0:1])
        fa, fb = jnp.exp2(stat_a[0:1] - top), jnp.exp2(stat_b[0:1] - top)
        total = stat_a[1:2] * fa + stat_b[1:2] * fb
        acc = acc_a.astype(jnp.float32) * fa + acc_b.astype(jnp.float32) * fb
        return acc, jnp.concatenate([top, total], axis=0)

    def arrived(dirn, c, k):
        for copy in flights[dirn, c, k]:
            copy.wait_recv()
        return acc_recv[dirn, c, k], stat_recv[dirn, c, k]

    def mine(d, c):
        target = wrap(w + d, side)
        return accs[target, :, cols(c)], stats[target, :, cols(c)]

    for k in range(half):
        for c in (0, 1):
            for dirn in (0, 1):
                reach = far(dirn, c) - k
                if reach < 1:
                    continue
                acc, stat = mine((1, -1)[dirn] * reach, c)
                if k > 0:
                    acc, stat = merge((acc, stat), arrived(dirn, c, k - 1))
                acc_send[dirn, c, k] = acc.astype(jnp.bfloat16)
                stat_send[dirn, c, k] = stat
                launch(dirn, c, k, acc_send.at[dirn, c, k], stat_send.at[dirn, c, k])

    exchange = []
    for c in (0, 1):
        total = mine(0, c)
        for dirn in (1, 0):
            total = merge(total, arrived(dirn, c, far(dirn, c) - 1))
        acc, stat = total
        final = acc / stat[1:2]
        for j in range(part // tokens):
            block = jnp.transpose(final[:, j * tokens : (j + 1) * tokens])
            at = c * part // tokens + j
            result[:, at * HD : (at + 1) * HD] = block.astype(result.dtype)
    width = result.shape[1]
    spot = pl.ds(pl.multiple_of(me * width, width), width)
    for hop in range(1, peers):
        peer = lax.rem(me + hop, peers)
        copy = pltpu.make_async_remote_copy(
            src_ref=result.at[pl.ds(pl.multiple_of(peer * share, share), share)],
            dst_ref=out.at[:, spot],
            send_sem=xsend.at[hop],
            recv_sem=xrecv.at[hop],
            device_id={"heads": peer},
            device_id_type=MESH,
        )
        copy.start()
        exchange.append(copy)
    keep = pltpu.make_async_copy(
        result.at[pl.ds(pl.multiple_of(me * share, share), share)], out.at[:, spot], xlocal
    )
    keep.start()
    for copy in exchange:
        copy.wait_recv()
    for copy in exchange:
        copy.wait_send()
    keep.wait()
    for copies in flights.values():
        for copy in copies:
            copy.wait_send()


def return_partials(acc_all, stat_all, side, peers):
    half = side // 2
    rows = acc_all.shape[2]
    tokens = rows // GROUP
    part = rows // 2
    width = GROUP * HD
    return pl.pallas_call(
        functools.partial(return_kernel, side),
        out_shape=jax.ShapeDtypeStruct((tokens // peers, peers * width), jnp.bfloat16),
        in_specs=[VMEM] * 2,
        out_specs=HBM,
        scratch_shapes=[
            pltpu.VMEM((2, 2, half, HD, part), jnp.bfloat16),
            pltpu.VMEM((2, 2, half, 2, part), jnp.float32),
            pltpu.VMEM((2, 2, half, HD, part), jnp.bfloat16),
            pltpu.VMEM((2, 2, half, 2, part), jnp.float32),
            pltpu.VMEM((tokens, width), jnp.bfloat16),
            pltpu.SemaphoreType.DMA((2, 2, half, 2)),
            pltpu.SemaphoreType.DMA((2, 2, half, 2)),
            pltpu.SemaphoreType.DMA((peers,)),
            pltpu.SemaphoreType.DMA((peers,)),
            pltpu.SemaphoreType.DMA,
        ],
        compiler_params=pltpu.CompilerParams(
            collective_id=1, has_side_effects=True, vmem_limit_bytes=16 << 20
        ),
        name="return_partials",
    )(acc_all, stat_all)


def per_device(
    queries,
    new_keys,
    new_values,
    library_keys,
    library_values,
    module_owner,
    module_page,
    module_count,
):
    rows_count = lax.axis_size("rows")
    peers = lax.axis_size("heads")
    side = math.isqrt(rows_count)
    k_all, v_all, q_all, table = gather_lines(
        module_owner, module_page, module_count, library_keys, library_values, queries, side
    )
    acc_all, stat_all = partials(table, q_all, new_keys, new_values, k_all, v_all, side)
    return return_partials(acc_all, stat_all, side, peers)


def solution(mesh):
    placed = (
        P("rows", "heads"),
        P("rows", "heads"),
        P("rows", "heads"),
        P("rows", None, "heads"),
        P("rows", None, "heads"),
        P("rows", None),
        P("rows", None),
        P("rows"),
    )
    return jax.shard_map(
        per_device,
        mesh=mesh,
        in_specs=placed,
        out_specs=P(("rows", "heads"), None),
        check_vma=False,
    )
```

time: 112 us -> 106 us (0.946)
  Pallas kernels: 110 us -> 104 us
    pallas_call x2, Pallas kernels: 80.7 us -> 71.9 us  [the longest x1 65.3 us: gather_lines(): pl.pallas_call(functools.partial(gather_kernel, side), out_shape=[pltpu.V...]
    pallas_call x1, Pallas kernels: 28.9 us -> 32.1 us  [return_partials(): pl.pallas_call(functools.partial(return_kernel, side), out_shape=jax.Shap...]
where the time goes in v3:
time: 106 us; the launch traced here: 105 us
  Pallas kernels  104 us (98%)
    pallas_call x1, Pallas kernels, gather_lines(): pl.pallas_call(functools.partial(gather_kernel, side), out_shape=[pltpu.V...  65.3 us
    pallas_call x1, Pallas kernels, return_partials(): pl.pallas_call(functools.partial(return_kernel, side), out_shape=jax.Shap...  32.1 us
    pallas_call x1, Pallas kernels, partials(): pl.pallas_call(functools.partial(partial_kernel, side), out_shape=[pltpu....  6.59 us

profile of v3, /device:TPU:1, one launch (start us, length us, event | category | flops | bytes accessed | tf_op | source)
XLA Modules:
  0.0 105.4 jit_solution(4016061634606691652)
XLA Ops:
  0.7 65.3 %gather_lines.1 = (bf16[8,16,128,128]{3,2,1,0:T(8,128)(2,1)S(1)}, bf16[8,16,128,128]{3,2,1,0:T(8,128)(2,1)S(1)}, bf16[8,128,1024]{2,1,0:T(8,128)(2,1)S(1)}, s32[8,8,128]{2,1,0:T(8,128)S(1)}) custom-call(s32[1,16]{1,0:T(1,128)} %owner_in.1, s32[1,16]{1,0:T(1,128)} %page_in.1, s32[1]{0:T(128)S(6)} %copy.10.count, bf16[16,128,128]{2,1,0:T(8,128)(2,1)} %k_in.1, ...), custom_call_target="tpu_custom_call" | custom-call | tf_op jit(solution)/shard_map/gather_lines/pallas_call | solution.py:153
  66.0 6.6 %partials.1 = (f32[8,128,1024]{2,1,0:T(8,128)S(1)}, f32[8,2,1024]{2,1,0:T(2,128)S(1)}) custom-call(s32[8,8,128]{2,1,0:T(8,128)S(1)} %get-tuple-element.11.table, bf16[128,128]{1,0:T(8,128)(2,1)} %nk_hbm.1, bf16[128,128]{1,0:T(8,128)(2,1)} %nv_hbm.1, bf16[8,128,1024]{2,1,0:T(8,128)(2,1)S(1)} %get-tuple-element.12.q_all, ...), custom_call_target="tpu_custom_call" | custom-call | tf_op jit(solution)/shard_map/partials/pallas_call | solution.py:234
  72.6 32.1 %return_partials.1 = bf16[16,8192]{1,0:T(8,128)(2,1)S(1)} custom-call(f32[8,128,1024]{2,1,0:T(8,128)S(1)} %get-tuple-element.15.accs, f32[8,2,1024]{2,1,0:T(2,128)S(1)} %get-tuple-element.16.stats), custom_call_target="tpu_custom_call" | custom-call | tf_op jit(solution)/shard_map/return_partials/pallas_call | solution.py:375
  104.7 0.7 copy.11

commit v4 on v3

--- a/solution.py
+++ b/solution.py
@@ -249,16 +249,15 @@
     )(table, in_hbm(nk), in_hbm(nv), q_all, k_all, v_all)
 
 
-def return_kernel(
-    side, accs, stats, out, acc_send, stat_send, acc_recv, stat_recv, result, send, recv, xsend, xrecv, xlocal
-):
+def return_kernel(side, accs, stats, out, outgoing, incoming, result, send, recv, xsend, xrecv, xlocal):
     core, u, w = place(side)
     me = lax.axis_index("heads")
     peers = lax.axis_size("heads")
     half = side // 2
-    rows = accs.shape[2]
-    part = rows // 2
-    tokens = result.shape[0]
+    chunks = outgoing.shape[1]
+    part = outgoing.shape[4]
+    extra = outgoing.shape[3] - HD
+    tokens, width = result.shape
     share = tokens // peers
     near = [row_of(core, u, wrap(w + d, side), side) for d in (1, -1)]
 
@@ -269,125 +268,139 @@
         pl.semaphore_signal(
             barrier, inc=1, device_id={"heads": lax.rem(me + hop, peers)}, device_id_type=MESH
         )
-    pl.semaphore_wait(barrier, 1 + peers)
-
-    def cols(c):
-        return slice(c * part, (c + 1) * part)
 
     def far(dirn, c):
-        return half if dirn == c else half - 1
+        return half if c % 2 == dirn else half - 1
+
+    def mine(d, c):
+        target, cols = wrap(w + d, side), slice(c * part, (c + 1) * part)
+        return accs[target, :, cols], stats[target, 0:1, cols], stats[target, 1:2, cols]
+
+    def split(value):
+        pieces = []
+        for _ in range(3):
+            pieces.append(value.astype(jnp.bfloat16).astype(jnp.float32))
+            value = value - pieces[-1]
+        return pieces
+
+    row_at = lax.broadcasted_iota(jnp.int32, (extra, part), 0)
+
+    def pack(ref, item):
+        acc, top, total = item
+        ref[0:HD] = acc.astype(jnp.bfloat16)
+        tail = jnp.zeros((extra, part), jnp.float32)
+        for i, piece in enumerate(split(top) + split(total)):
+            tail = jnp.where(row_at == i, piece, tail)
+        ref[HD : HD + extra] = tail.astype(jnp.bfloat16)
+
+    def unpack(ref):
+        tail = ref[HD : HD + extra].astype(jnp.float32)
+        top = tail[0:1] + tail[1:2] + tail[2:3]
+        total = tail[3:4] + tail[4:5] + tail[5:6]
+        return ref[0:HD].astype(jnp.float32), top, total
+
+    def merge(one, two):
+        top = jnp.maximum(one[1], two[1])
+        fa, fb = jnp.exp2(one[1] - top), jnp.exp2(two[1] - top)
+        return one[0] * fa + two[0] * fb, top, one[2] * fa + two[2] * fb
 
     flights = {}
 
-    def launch(dirn, c, k, acc_src, stat_src):
-        copies = [
-            pltpu.make_async_remote_copy(
-                src_ref=src,
-                dst_ref=dst,
-                send_sem=send.at[dirn, c, k, kind],
-                recv_sem=recv.at[dirn, c, k, kind],
-                device_id={"rows": near[dirn]},
-                device_id_type=MESH,
-            )
-            for kind, (src, dst) in enumerate(
-                [(stat_src, stat_recv.at[dirn, c, k]), (acc_src, acc_recv.at[dirn, c, k])]
-            )
-        ]
-        for copy in copies:
-            copy.start()
-        flights[dirn, c, k] = copies
-
-    def merge(one, two):
-        (acc_a, stat_a), (acc_b, stat_b) = one, two
-        top = jnp.maximum(stat_a[0:1], stat_b[0:1])
-        fa, fb = jnp.exp2(stat_a[0:1] - top), jnp.exp2(stat_b[0:1] - top)
-        total = stat_a[1:2] * fa + stat_b[1:2] * fb
-        acc = acc_a.astype(jnp.float32) * fa + acc_b.astype(jnp.float32) * fb
-        return acc, jnp.concatenate([top, total], axis=0)
-
-    def arrived(dirn, c, k):
-        for copy in flights[dirn, c, k]:
-            copy.wait_recv()
-        return acc_recv[dirn, c, k], stat_recv[dirn, c, k]
-
-    def mine(d, c):
-        target = wrap(w + d, side)
-        return accs[target, :, cols(c)], stats[target, :, cols(c)]
-
-    for k in range(half):
-        for c in (0, 1):
-            for dirn in (0, 1):
-                reach = far(dirn, c) - k
-                if reach < 1:
-                    continue
-                acc, stat = mine((1, -1)[dirn] * reach, c)
-                if k > 0:
-                    acc, stat = merge((acc, stat), arrived(dirn, c, k - 1))
-                acc_send[dirn, c, k] = acc.astype(jnp.bfloat16)
-                stat_send[dirn, c, k] = stat
-                launch(dirn, c, k, acc_send.at[dirn, c, k], stat_send.at[dirn, c, k])
-
-    exchange = []
-    for c in (0, 1):
-        total = mine(0, c)
-        for dirn in (1, 0):
-            total = merge(total, arrived(dirn, c, far(dirn, c) - 1))
-        acc, stat = total
-        final = acc / stat[1:2]
-        for j in range(part // tokens):
-            block = jnp.transpose(final[:, j * tokens : (j + 1) * tokens])
-            at = c * part // tokens + j
-            result[:, at * HD : (at + 1) * HD] = block.astype(result.dtype)
-    width = result.shape[1]
-    spot = pl.ds(pl.multiple_of(me * width, width), width)
-    for hop in range(1, peers):
-        peer = lax.rem(me + hop, peers)
+    def launch(dirn, c, k):
         copy = pltpu.make_async_remote_copy(
-            src_ref=result.at[pl.ds(pl.multiple_of(peer * share, share), share)],
-            dst_ref=out.at[:, spot],
-            send_sem=xsend.at[hop],
-            recv_sem=xrecv.at[hop],
-            device_id={"heads": peer},
+            src_ref=outgoing.at[dirn, c, k],
+            dst_ref=incoming.at[dirn, c, k],
+            send_sem=send.at[dirn, c, k],
+            recv_sem=recv.at[dirn, c, k],
+            device_id={"rows": near[dirn]},
             device_id_type=MESH,
         )
         copy.start()
-        exchange.append(copy)
-    keep = pltpu.make_async_copy(
-        result.at[pl.ds(pl.multiple_of(me * share, share), share)], out.at[:, spot], xlocal
-    )
-    keep.start()
+        flights[dirn, c, k] = copy
+
+    def arrived(dirn, c, k):
+        flights[dirn, c, k].wait_recv()
+        return unpack(incoming.at[dirn, c, k])
+
+    starts = [(c, dirn) for c in range(chunks) for dirn in (0, 1)]
+    for c, dirn in starts:
+        pack(outgoing.at[dirn, c, 0], mine((1, -1)[dirn] * far(dirn, c), c))
+    pl.semaphore_wait(barrier, 1 + peers)
+    for c, dirn in starts:
+        launch(dirn, c, 0)
+    for k in range(1, half):
+        for c, dirn in starts:
+            reach = far(dirn, c) - k
+            if reach < 1:
+                continue
+            item = mine((1, -1)[dirn] * reach, c)
+            pack(outgoing.at[dirn, c, k], merge(item, arrived(dirn, c, k - 1)))
+            launch(dirn, c, k)
+
+    exchange = []
+    groups = exchange_groups(chunks)
+    for g, group in enumerate(groups):
+        for c in group:
+            item = mine(0, c)
+            for dirn in sorted((0, 1), key=lambda dirn: far(dirn, c)):
+                item = merge(item, arrived(dirn, c, far(dirn, c) - 1))
+            final = item[0] / item[2]
+            for j in range(part // tokens):
+                at = c * part // tokens + j
+                block = jnp.transpose(final[:, j * tokens : (j + 1) * tokens])
+                result[:, at * HD : (at + 1) * HD] = block.astype(result.dtype)
+        first, size = group[0] * part, len(group) * part
+        here = slice(first, first + size)
+        there = pl.ds(pl.multiple_of(me * width + first, size), size)
+        for hop in range(1, peers):
+            peer = lax.rem(me + hop, peers)
+            copy = pltpu.make_async_remote_copy(
+                src_ref=result.at[pl.ds(pl.multiple_of(peer * share, share), share), here],
+                dst_ref=out.at[:, there],
+                send_sem=xsend.at[g, hop],
+                recv_sem=xrecv.at[g, hop],
+                device_id={"heads": peer},
+                device_id_type=MESH,
+            )
+            copy.start()
+            exchange.append(copy)
+        keep = pltpu.make_async_copy(
+            result.at[pl.ds(pl.multiple_of(me * share, share), share), here], out.at[:, there], xlocal.at[g]
+        )
+        keep.start()
+        exchange.append(keep)
     for copy in exchange:
-        copy.wait_recv()
-    for copy in exchange:
+        copy.wait()
+    for copy in flights.values():
         copy.wait_send()
-    keep.wait()
-    for copies in flights.values():
-        for copy in copies:
-            copy.wait_send()
+
+
+def exchange_groups(chunks):
+    return [list(range(chunks))[i : i + chunks // 2] for i in (0, chunks // 2)]
 
 
 def return_partials(acc_all, stat_all, side, peers):
     half = side // 2
     rows = acc_all.shape[2]
     tokens = rows // GROUP
-    part = rows // 2
+    chunks = 4
     width = GROUP * HD
+    groups = len(exchange_groups(chunks))
+    message = (2, chunks, half, HD + 8, rows // chunks)
     return pl.pallas_call(
         functools.partial(return_kernel, side),
         out_shape=jax.ShapeDtypeStruct((tokens // peers, peers * width), jnp.bfloat16),
         in_specs=[VMEM] * 2,
         out_specs=HBM,
         scratch_shapes=[
-            pltpu.VMEM((2, 2, half, HD, part), jnp.bfloat16),
-            pltpu.VMEM((2, 2, half, 2, part), jnp.float32),
-            pltpu.VMEM((2, 2, half, HD, part), jnp.bfloat16),
-            pltpu.VMEM((2, 2, half, 2, part), jnp.float32),
+            pltpu.VMEM(message, jnp.bfloat16),
+            pltpu.VMEM(message, jnp.bfloat16),
             pltpu.VMEM((tokens, width), jnp.bfloat16),
-            pltpu.SemaphoreType.DMA((2, 2, half, 2)),
-            pltpu.SemaphoreType.DMA((2, 2, half, 2)),
-            pltpu.SemaphoreType.DMA((peers,)),
-            pltpu.SemaphoreType.DMA((peers,)),
-            pltpu.SemaphoreType.DMA,
+            pltpu.SemaphoreType.DMA((2, chunks, half)),
+            pltpu.SemaphoreType.DMA((2, chunks, half)),
+            pltpu.SemaphoreType.DMA((groups, peers)),
+            pltpu.SemaphoreType.DMA((groups, peers)),
+            pltpu.SemaphoreType.DMA((groups,)),
         ],
         compiler_params=pltpu.CompilerParams(
             collective_id=1, has_side_effects=True, vmem_limit_bytes=16 << 20

time: 106 us -> 103 us (0.972)
  Pallas kernels: 104 us -> 101 us
    pallas_call x1, Pallas kernels: 32.1 us -> 26.3 us  [return_partials(): pl.pallas_call(functools.partial(return_kernel, side), out_shape=jax.Shap...]
    pallas_call x1, Pallas kernels: 6.59 us -> 9.4 us  [partials(): pl.pallas_call(functools.partial(partial_kernel, side), out_shape=[pltpu....]
where the time goes in v4:
time: 103 us; the launch traced here: 102 us
  Pallas kernels  101 us (98%)
    pallas_call x1, Pallas kernels, gather_lines(): pl.pallas_call(functools.partial(gather_kernel, side), out_shape=[pltpu.V...  65.3 us
    pallas_call x1, Pallas kernels, return_partials(): pl.pallas_call(functools.partial(return_kernel, side), out_shape=jax.Shap...  26.3 us
    pallas_call x1, Pallas kernels, partials(): pl.pallas_call(functools.partial(partial_kernel, side), out_shape=[pltpu....  9.4 us

profile of v4, /device:TPU:1, one launch (start us, length us, event | category | flops | bytes accessed | tf_op | source)
XLA Modules:
  0.0 102.4 jit_solution(10776316360942637046)
XLA Ops:
  0.7 65.3 %gather_lines.1 = (bf16[8,16,128,128]{3,2,1,0:T(8,128)(2,1)S(1)}, bf16[8,16,128,128]{3,2,1,0:T(8,128)(2,1)S(1)}, bf16[8,128,1024]{2,1,0:T(8,128)(2,1)S(1)}, s32[8,8,128]{2,1,0:T(8,128)S(1)}) custom-call(s32[1,16]{1,0:T(1,128)} %owner_in.1, s32[1,16]{1,0:T(1,128)} %page_in.1, s32[1]{0:T(128)S(6)} %copy.10.count, bf16[16,128,128]{2,1,0:T(8,128)(2,1)} %k_in.1, ...), custom_call_target="tpu_custom_call" | custom-call | tf_op jit(solution)/shard_map/gather_lines/pallas_call | solution.py:153
  66.0 9.4 %partials.1 = (f32[8,128,1024]{2,1,0:T(8,128)S(1)}, f32[8,2,1024]{2,1,0:T(2,128)S(1)}) custom-call(s32[8,8,128]{2,1,0:T(8,128)S(1)} %get-tuple-element.11.table, bf16[128,128]{1,0:T(8,128)(2,1)} %nk_hbm.1, bf16[128,128]{1,0:T(8,128)(2,1)} %nv_hbm.1, bf16[8,128,1024]{2,1,0:T(8,128)(2,1)S(1)} %get-tuple-element.12.q_all, ...), custom_call_target="tpu_custom_call" | custom-call | tf_op jit(solution)/shard_map/partials/pallas_call | solution.py:234
  75.4 26.3 %return_partials.1 = bf16[16,8192]{1,0:T(8,128)(2,1)S(1)} custom-call(f32[8,128,1024]{2,1,0:T(8,128)S(1)} %get-tuple-element.15.accs, f32[8,2,1024]{2,1,0:T(2,128)S(1)} %get-tuple-element.16.stats), custom_call_target="tpu_custom_call" | custom-call | tf_op jit(solution)/shard_map/return_partials/pallas_call | solution.py:390
  101.7 0.7 copy.11

commit v5 on v4

--- a/solution.py
+++ b/solution.py
@@ -15,6 +15,7 @@
 MESH = pl.DeviceIdType.MESH
 LOG2E = 1.4426950408889634
 FLOOR = -1e30
+NEAR_SLOTS = 3
 
 
 def place(side):
@@ -34,13 +35,47 @@
     return lax.rem(value + 4 * side, side)
 
 
+def accumulate(acc, stat, q_all, req, keys, values, live=None, causal=False):
+    scale = LOG2E / math.sqrt(HD)
+    rows = q_all.shape[2]
+    tokens = rows // GROUP
+    wide = 2 * tokens
+    for c in range(rows // wide):
+        cols = slice(c * wide, (c + 1) * wide)
+        raw = jnp.dot(keys, q_all[req, :, cols], preferred_element_type=jnp.float32)
+        if causal:
+            key_at = lax.broadcasted_iota(jnp.int32, raw.shape, 0)
+            token_at = lax.rem(lax.broadcasted_iota(jnp.int32, raw.shape, 1), tokens)
+            allowed = key_at <= token_at
+            raw = jnp.where(allowed, raw, FLOOR)
+        old = stat[req, 0:1, cols]
+        high = jnp.max(raw, axis=0, keepdims=True) * scale
+        if live is not None:
+            high = jnp.where(live, high, FLOOR)
+        top = jnp.maximum(old, high)
+        base = top if live is None else jnp.where(live, top, -FLOOR)
+        weights = jnp.exp2(raw * scale - base)
+        if causal:
+            weights = jnp.where(allowed, weights, 0.0)
+        shrink = jnp.exp2(old - top)
+        stat[req, 0:1, cols] = top
+        stat[req, 1:2, cols] = stat[req, 1:2, cols] * shrink + jnp.sum(weights, axis=0, keepdims=True)
+        mixed = jnp.dot(values, weights.astype(jnp.bfloat16), preferred_element_type=jnp.float32)
+        acc[req, :, cols] = acc[req, :, cols] * shrink + mixed
+
+
 def gather_kernel(
-    side, owner_in, page_in, count, k_in, v_in, q_in, k_all, v_all, q_all, t_all, owner, page, vraw, qraw, send, recv, local
+    side,
+    owner_in, page_in, count, k_in, v_in, q_in, nk_in, nv_in,
+    k_near, v_near, k_far, v_far, q_all, t_all, acc, stat,
+    owner, page, table, vraw, qraw, nk, nv, send, recv, local,
 ):
     core, u, w = place(side)
     half = side // 2
+    reach = k_near.shape[0] // 2
     heads_wide = q_all.shape[2] // 2
     shape = t_all.shape[1:]
+    middle = shape[1] // 2
     slots = owner.shape[1]
     pages = k_in.shape[0]
     tokens = qraw.shape[0]
@@ -50,39 +85,45 @@
     barrier = pltpu.get_barrier_semaphore()
     for row in lib_at + que_at:
         pl.semaphore_signal(barrier, inc=1, device_id={"rows": row}, device_id_type=MESH)
-    fetch_q = pltpu.make_async_copy(q_in, qraw, local.at[4])
-    fetch_v = pltpu.make_async_copy(v_in, vraw, local.at[5])
-    lists = [
-        pltpu.make_async_copy(owner_in, owner, local.at[1]),
-        pltpu.make_async_copy(page_in, page, local.at[2]),
-    ]
-    for copy in lists:
+
+    def fetch(at, src, dst):
+        copy = pltpu.make_async_copy(src, dst, local.at[at])
         copy.start()
-    fetch_q.start()
-    fetch_v.start()
-    own = [pltpu.make_async_copy(k_in, k_all.at[u], local.at[0])]
-    own[0].start()
-
+        return copy
+
+    lists = [fetch(0, owner_in, owner), fetch(1, page_in, page)]
+    fetch_q, fetch_v = fetch(2, q_in, qraw), fetch(3, v_in, vraw)
+    own_k = fetch(4, k_in, k_near.at[reach])
+    fresh = [fetch(5, nk_in, nk), fetch(6, nv_in, nv)]
     pl.semaphore_wait(barrier, 4)
+
+    def shard(kind, d):
+        near, far = ((k_near, k_far), (v_near, v_far))[kind]
+        if abs(d) <= reach:
+            return near.at[d + reach]
+        return far.at[d % side - reach - 1]
+
     started = {}
     waited = set()
 
+    def receive(key):
+        if key not in waited:
+            started[key].wait_recv()
+            waited.add(key)
+
     def start(dirn, step, kind):
         sign = (1, -1)[dirn]
-        u0, w0 = wrap(u - sign * step, side), wrap(w - sign * step, side)
         if step > 0:
-            started[dirn, step - 1, kind].wait_recv()
-            waited.add((dirn, step - 1, kind))
-        all_ref, row = (
-            (k_all.at[u0], lib_at[dirn]),
-            (v_all.at[u0], lib_at[dirn]),
-            (q_all.at[w0], que_at[dirn]),
-            (t_all.at[w0], que_at[dirn]),
-        )[kind]
-        src, dst = (k_in if step == 0 and kind == 0 else all_ref), all_ref
-        if kind == 2 and step == half - 1:
-            cols = pl.ds(dirn * heads_wide, heads_wide)
-            src, dst = all_ref.at[:, cols], all_ref.at[:, cols]
+            receive((dirn, step - 1, kind))
+        if kind < 2:
+            src = k_in if step == 0 and kind == 0 else shard(kind, -sign * step)
+            dst, row = shard(kind, -sign * (step + 1)), lib_at[dirn]
+        else:
+            w0 = wrap(w - sign * step, side)
+            dst, row = (q_all.at[w0], t_all.at[w0])[kind - 2], que_at[dirn]
+            if kind == 2 and step == half - 1:
+                dst = dst.at[:, pl.ds(dirn * heads_wide, heads_wide)]
+            src = dst
         copy = pltpu.make_async_remote_copy(
             src_ref=src,
             dst_ref=dst,
@@ -94,48 +135,85 @@
         copy.start()
         started[dirn, step, kind] = copy
 
-    for dirn in (0, 1):
-        start(dirn, 0, 0)
+    def both(step, kind):
+        for dirn in (0, 1):
+            start(dirn, step, kind)
+
+    both(0, 0)
     for copy in lists:
         copy.wait()
     line_at = lax.broadcasted_iota(jnp.int32, shape, 0)
     lane_at = lax.broadcasted_iota(jnp.int32, shape, 1)
-    filled = jnp.zeros(shape, jnp.int32)
+    filled = [jnp.zeros(shape, jnp.int32), jnp.full(shape, middle, jnp.int32)]
     packed = jnp.zeros(shape, jnp.int32)
     for slot in range(slots):
         z, y = owner[0, slot] // side, lax.rem(owner[0, slot], side)
         line = (1 - core) * z + core * y
         cross = (1 - core) * y + core * z
-        hit = jnp.logical_and(line_at == cross, count[0] > slot)
-        packed = jnp.where(jnp.logical_and(hit, lane_at == filled), line * pages + page[0, slot], packed)
-        filled = filled + jnp.where(hit, 1, 0)
-    t_all[w] = jnp.where(lane_at == shape[1] - 1, filled, packed)
-    for dirn in (0, 1):
-        start(dirn, 0, 3)
+        ahead = wrap(line - u + reach, side)
+        listed = jnp.logical_and(line_at == cross, count[0] > slot)
+        for far in (0, 1):
+            hit = jnp.logical_and(listed, (ahead > 2 * reach) if far else (ahead <= 2 * reach))
+            spot = (ahead - far * (2 * reach + 1)) * pages + page[0, slot]
+            packed = jnp.where(jnp.logical_and(hit, lane_at == filled[far]), spot, packed)
+            filled[far] = filled[far] + jnp.where(hit, 1, 0)
+    packed = jnp.where(lane_at == middle - 1, filled[0], packed)
+    t_all[w] = jnp.where(lane_at == shape[1] - 1, filled[1] - middle, packed)
+    both(0, 3)
     fetch_q.wait()
     for j in range(GROUP):
         q_all[w, :, j * tokens : (j + 1) * tokens] = jnp.transpose(qraw[:, j * HD : (j + 1) * HD])
-    for dirn in (0, 1):
-        start(dirn, 0, 2)
+    both(0, 2)
     fetch_v.wait()
     for j in range(pages):
-        v_all[u, j] = jnp.transpose(vraw[j])
+        v_near[reach, j] = jnp.transpose(vraw[j])
+    both(0, 1)
+    for step in range(1, half - 1):
+        both(step, 3)
+    start(0, half - 1, 3)
+
+    @pl.loop(0, side)
+    def _(req):
+        acc[req] = jnp.zeros(acc.shape[1:], jnp.float32)
+        stat[req, 0:1] = jnp.full((1, acc.shape[2]), FLOOR, jnp.float32)
+        stat[req, 1:2] = jnp.zeros((1, acc.shape[2]), jnp.float32)
+
+    for copy in fresh:
+        copy.wait()
+    accumulate(acc, stat, q_all, w, nk[...], jnp.transpose(nv[...]), causal=True)
+    receive((0, half - 1, 3))
+    receive((1, half - 2, 3))
+    to_scalars = fetch(7, t_all, table)
+
+    both(1, 0)
+    both(1, 2)
+    both(1, 1)
+    both(2, 2)
+    both(2, 0)
+    both(3, 2)
+    both(2, 1)
     for dirn in (0, 1):
-        start(dirn, 0, 1)
-    for step in range(1, half):
-        last = step == half - 1
-        for kind in (3, 0, 2, 1):
-            for dirn in (0, 1):
-                if last and (dirn, kind) in ((1, 0), (0, 1), (1, 3)):
-                    continue
-                start(dirn, step, kind)
-    for key, copy in started.items():
-        if key not in waited:
-            copy.wait_recv()
+        receive((dirn, half - 1, 2))
+    own_k.wait()
+    to_scalars.wait()
+
+    def listed_near(first, last):
+        @pl.loop(first * NEAR_SLOTS, last * NEAR_SLOTS)
+        def _(at):
+            req, k = at // NEAR_SLOTS, lax.rem(at, NEAR_SLOTS)
+            live = k < table[req, w, middle - 1]
+            spot = table[req, w, k]
+            line, page_at = spot // pages, lax.rem(spot, pages)
+            accumulate(acc, stat, q_all, req, k_near[line, page_at], v_near[line, page_at], live=live)
+
+    listed_near(0, half)
+    start(0, half - 1, 0)
+    start(1, half - 1, 1)
+    listed_near(half, side)
+    for key in started:
+        receive(key)
     for copy in started.values():
         copy.wait_send()
-    for copy in own:
-        copy.wait()
 
 
 HBM = pl.BlockSpec(memory_space=pltpu.HBM)
@@ -147,106 +225,75 @@
     return pltpu.with_memory_space_constraint(a, pltpu.HBM)
 
 
-def gather_lines(owner, page, count, k, v, q, side):
+def gather_lines(owner, page, count, k, v, q, nk, nv, side):
     half = side // 2
     tokens = q.shape[0]
+    near, far = 2 * (half - 2) + 1, side - 2 * (half - 2) - 1
     return pl.pallas_call(
         functools.partial(gather_kernel, side),
         out_shape=[
-            pltpu.VMEM((side,) + k.shape, k.dtype),
-            pltpu.VMEM((side,) + v.shape, v.dtype),
+            pltpu.VMEM((near,) + k.shape, k.dtype),
+            pltpu.VMEM((near,) + v.shape, v.dtype),
+            pltpu.VMEM((far,) + k.shape, k.dtype),
+            pltpu.VMEM((far,) + v.shape, v.dtype),
             pltpu.VMEM((side, HD, GROUP * tokens), q.dtype),
             pltpu.VMEM((side, side, 128), jnp.int32),
+            pltpu.VMEM((side, HD, GROUP * tokens), jnp.float32),
+            pltpu.VMEM((side, 2, GROUP * tokens), jnp.float32),
         ],
-        in_specs=[HBM, HBM, SMEM, HBM, HBM, HBM],
-        out_specs=[VMEM] * 4,
+        in_specs=[HBM, HBM, SMEM] + [HBM] * 5,
+        out_specs=[VMEM] * 8,
         scratch_shapes=[
             pltpu.SMEM(owner.shape, owner.dtype),
             pltpu.SMEM(page.shape, page.dtype),
+            pltpu.SMEM((side, side, 128), jnp.int32),
             pltpu.VMEM(v.shape, v.dtype),
             pltpu.VMEM(q.shape, q.dtype),
+            pltpu.VMEM(nk.shape, nk.dtype),
+            pltpu.VMEM(nv.shape, nv.dtype),
             pltpu.SemaphoreType.DMA((2, half, 4)),
             pltpu.SemaphoreType.DMA((2, half, 4)),
-            pltpu.SemaphoreType.DMA((6,)),
+            pltpu.SemaphoreType.DMA((8,)),
         ],
         compiler_params=pltpu.CompilerParams(
             collective_id=0, has_side_effects=True, vmem_limit_bytes=16 << 20
         ),
         name="gather_lines",
-    )(in_hbm(owner), in_hbm(page), count, in_hbm(k), in_hbm(v), in_hbm(q))
-
-
-def partial_kernel(side, table, nk_hbm, nv_hbm, q_all, k_all, v_all, acc, stat, nk, nv, fetched):
+    )(in_hbm(owner), in_hbm(page), count, *[in_hbm(a) for a in (k, v, q, nk, nv)])
+
+
+def partial_kernel(side, table, k_near, v_near, k_far, v_far, q_all, acc_in, stat_in, acc, stat):
+    del acc_in, stat_in
     _, _, w = place(side)
-    pages = k_all.shape[1]
-    scale = LOG2E / math.sqrt(HD)
-    rows = q_all.shape[2]
-    tokens = nk.shape[0]
-    wide = 2 * tokens
-    chunks = [slice(c * wide, (c + 1) * wide) for c in range(rows // wide)]
-    fetches = [
-        pltpu.make_async_copy(nk_hbm, nk, fetched.at[0]),
-        pltpu.make_async_copy(nv_hbm, nv, fetched.at[1]),
-    ]
-    for copy in fetches:
-        copy.start()
-
-    def dot(one, two):
-        return jnp.dot(one, two, preferred_element_type=jnp.float32)
-
-    def add(req, keys, values, causal):
-        for cols in chunks:
-            raw = dot(keys, q_all[req, :, cols])
-            if causal:
-                key_at = lax.broadcasted_iota(jnp.int32, raw.shape, 0)
-                token_at = lax.rem(lax.broadcasted_iota(jnp.int32, raw.shape, 1), tokens)
-                allowed = key_at <= token_at
-                raw = jnp.where(allowed, raw, FLOOR)
-            old = stat[req, 0:1, cols]
-            top = jnp.maximum(old, jnp.max(raw, axis=0, keepdims=True) * scale)
-            weights = jnp.exp2(raw * scale - top)
-            if causal:
-                weights = jnp.where(allowed, weights, 0.0)
-            shrink = jnp.exp2(old - top)
-            stat[req, 0:1, cols] = top
-            stat[req, 1:2, cols] = stat[req, 1:2, cols] * shrink + jnp.sum(weights, axis=0, keepdims=True)
-            acc[req, :, cols] = acc[req, :, cols] * shrink + dot(values, weights.astype(jnp.bfloat16))
+    pages = k_near.shape[1]
+    lanes = table.shape[2]
+    middle = lanes // 2
 
     @pl.loop(0, side)
     def _(req):
-        acc[req] = jnp.zeros((HD, rows), jnp.float32)
-        stat[req, 0:1] = jnp.full((1, rows), FLOOR, jnp.float32)
-        stat[req, 1:2] = jnp.zeros((1, rows), jnp.float32)
-
-        @pl.loop(0, table[req, w, table.shape[2] - 1])
+        @pl.loop(NEAR_SLOTS, jnp.maximum(table[req, w, middle - 1], NEAR_SLOTS))
         def _(k):
-            value = table[req, w, k]
-            line, page = value // pages, lax.rem(value, pages)
-            add(req, k_all[line, page], v_all[line, page], False)
-
-    for copy in fetches:
-        copy.wait()
-    add(w, nk[...], jnp.transpose(nv[...]), True)
-
-
-def partials(table, q_all, nk, nv, k_all, v_all, side):
-    rows = q_all.shape[2]
+            spot = table[req, w, k]
+            line, page = spot // pages, lax.rem(spot, pages)
+            accumulate(acc, stat, q_all, req, k_near[line, page], v_near[line, page])
+
+        @pl.loop(0, table[req, w, lanes - 1])
+        def _(k):
+            spot = table[req, w, middle + k]
+            line, page = spot // pages, lax.rem(spot, pages)
+            accumulate(acc, stat, q_all, req, k_far[line, page], v_far[line, page])
+
+
+def partials(table, k_near, v_near, k_far, v_far, q_all, acc, stat, side):
     return pl.pallas_call(
         functools.partial(partial_kernel, side),
-        out_shape=[
-            pltpu.VMEM((side, HD, rows), jnp.float32),
-            pltpu.VMEM((side, 2, rows), jnp.float32),
-        ],
-        in_specs=[SMEM, HBM, HBM, VMEM, VMEM, VMEM],
+        out_shape=[pltpu.VMEM(acc.shape, acc.dtype), pltpu.VMEM(stat.shape, stat.dtype)],
+        in_specs=[SMEM] + [VMEM] * 7,
         out_specs=[VMEM, VMEM],
-        scratch_shapes=[
-            pltpu.VMEM(nk.shape, nk.dtype),
-            pltpu.VMEM(nv.shape, nv.dtype),
-            pltpu.SemaphoreType.DMA((2,)),
-        ],
+        input_output_aliases={6: 0, 7: 1},
         compiler_params=pltpu.CompilerParams(vmem_limit_bytes=16 << 20),
         name="partials",
-    )(table, in_hbm(nk), in_hbm(nv), q_all, k_all, v_all)
+    )(table, k_near, v_near, k_far, v_far, q_all, acc, stat)
 
 
 def return_kernel(side, accs, stats, out, outgoing, incoming, result, send, recv, xsend, xrecv, xlocal):
@@ -422,10 +469,18 @@
     rows_count = lax.axis_size("rows")
     peers = lax.axis_size("heads")
     side = math.isqrt(rows_count)
-    k_all, v_all, q_all, table = gather_lines(
-        module_owner, module_page, module_count, library_keys, library_values, queries, side
+    *shards, q_all, table, acc, stat = gather_lines(
+        module_owner,
+        module_page,
+        module_count,
+        library_keys,
+        library_values,
+        queries,
+        new_keys,
+        new_values,
+        side,
     )
-    acc_all, stat_all = partials(table, q_all, new_keys, new_values, k_all, v_all, side)
+    acc_all, stat_all = partials(table, *shards, q_all, acc, stat, side)
     return return_partials(acc_all, stat_all, side, peers)
 
 

time: 103 us -> 98.2 us (0.953)
  Pallas kernels: 101 us -> 96.7 us
    pallas_call x1, Pallas kernels: 9.4 us -> 3.16 us  [partials(): pl.pallas_call(functools.partial(partial_kernel, side), out_shape=[pltpu....]
    pallas_call x1, Pallas kernels: 26.3 us -> 28.2 us  [return_partials(): pl.pallas_call(functools.partial(return_kernel, side), out_shape=jax.Shap...]
where the time goes in v5:
time: 98.2 us; the launch traced here: 98 us
  Pallas kernels  96.7 us (98%)
    pallas_call x1, Pallas kernels, gather_lines(): pl.pallas_call(functools.partial(gather_kernel, side), out_shape=[pltpu.V...  65.3 us
    pallas_call x1, Pallas kernels, return_partials(): pl.pallas_call(functools.partial(return_kernel, side), out_shape=jax.Shap...  28.2 us
    pallas_call x1, Pallas kernels, partials(): pl.pallas_call(functools.partial(partial_kernel, side), out_shape=[pltpu....  3.16 us

profile of v5, /device:TPU:1, one launch (start us, length us, event | category | flops | bytes accessed | tf_op | source)
XLA Modules:
  0.0 98.0 jit_solution(4460617845472170262)
XLA Ops:
  0.7 65.3 %gather_lines.1 = (bf16[5,16,128,128]{3,2,1,0:T(8,128)(2,1)S(1)}, bf16[5,16,128,128]{3,2,1,0:T(8,128)(2,1)S(1)}, bf16[3,16,128,128]{3,2,1,0:T(8,128)(2,1)S(1)}, ...) custom-call(s32[1,16]{1,0:T(1,128)} %owner_in.1, ...), custom_call_target="tpu_custom_call" | custom-call | tf_op jit(solution)/shard_map/gather_lines/pallas_call | solution.py:232
  66.0 3.2 %partials.1 = (f32[8,128,1024]{2,1,0:T(8,128)S(1)}, f32[8,2,1024]{2,1,0:T(2,128)S(1)}) custom-call(s32[8,8,128]{2,1,0:T(8,128)S(1)} %get-tuple-element.15.table, bf16[5,16,128,128]{3,2,1,0:T(8,128)(2,1)S(1)} %get-tuple-element.16.k_near, bf16[5,16,128,128]{3,2,1,0:T(8,128)(2,1)S(1)} %get-tuple-element.17.v_near, ...), custom_call_target="tpu_custom_call", output_to_operand_aliasing={{0}: (6, {}), {1}: (7, {})} | custom-call | tf_op jit(solution)/shard_map/partials/pallas_call | solution.py:288
  69.2 28.2 %return_partials.1 = bf16[16,8192]{1,0:T(8,128)(2,1)S(1)} custom-call(f32[8,128,1024]{2,1,0:T(8,128)S(1)} %get-tuple-element.23.accs, f32[8,2,1024]{2,1,0:T(2,128)S(1)} %get-tuple-element.24.stats), custom_call_target="tpu_custom_call" | custom-call | tf_op jit(solution)/shard_map/return_partials/pallas_call | solution.py:437
  97.3 0.7 copy.15

commit v6 on v5

--- a/solution.py
+++ b/solution.py
@@ -16,6 +16,8 @@
 LOG2E = 1.4426950408889634
 FLOOR = -1e30
 NEAR_SLOTS = 3
+MID_SLOTS = 2
+UNROLL = True
 
 
 def place(side):
@@ -35,39 +37,44 @@
     return lax.rem(value + 4 * side, side)
 
 
-def accumulate(acc, stat, q_all, req, keys, values, live=None, causal=False):
+def accumulate(acc, stat, q_all, req, items, causal=False):
     scale = LOG2E / math.sqrt(HD)
     rows = q_all.shape[2]
     tokens = rows // GROUP
     wide = 2 * tokens
     for c in range(rows // wide):
         cols = slice(c * wide, (c + 1) * wide)
-        raw = jnp.dot(keys, q_all[req, :, cols], preferred_element_type=jnp.float32)
+        query = q_all[req, :, cols]
+        raws = [jnp.dot(keys, query, preferred_element_type=jnp.float32) for keys, _, _ in items]
         if causal:
-            key_at = lax.broadcasted_iota(jnp.int32, raw.shape, 0)
-            token_at = lax.rem(lax.broadcasted_iota(jnp.int32, raw.shape, 1), tokens)
+            key_at = lax.broadcasted_iota(jnp.int32, raws[0].shape, 0)
+            token_at = lax.rem(lax.broadcasted_iota(jnp.int32, raws[0].shape, 1), tokens)
             allowed = key_at <= token_at
-            raw = jnp.where(allowed, raw, FLOOR)
+            raws = [jnp.where(allowed, raw, FLOOR) for raw in raws]
         old = stat[req, 0:1, cols]
-        high = jnp.max(raw, axis=0, keepdims=True) * scale
-        if live is not None:
-            high = jnp.where(live, high, FLOOR)
-        top = jnp.maximum(old, high)
-        base = top if live is None else jnp.where(live, top, -FLOOR)
-        weights = jnp.exp2(raw * scale - base)
-        if causal:
-            weights = jnp.where(allowed, weights, 0.0)
+        top = old
+        for raw, (_, _, live) in zip(raws, items):
+            high = jnp.max(raw, axis=0, keepdims=True) * scale
+            top = jnp.maximum(top, high if live is None else jnp.where(live, high, FLOOR))
         shrink = jnp.exp2(old - top)
+        total = stat[req, 1:2, cols] * shrink
+        mixed = acc[req, :, cols] * shrink
+        for raw, (_, values, live) in zip(raws, items):
+            base = top if live is None else jnp.where(live, top, -FLOOR)
+            weights = jnp.exp2(raw * scale - base)
+            if causal:
+                weights = jnp.where(allowed, weights, 0.0)
+            total = total + jnp.sum(weights, axis=0, keepdims=True)
+            mixed = mixed + jnp.dot(values, weights.astype(jnp.bfloat16), preferred_element_type=jnp.float32)
         stat[req, 0:1, cols] = top
-        stat[req, 1:2, cols] = stat[req, 1:2, cols] * shrink + jnp.sum(weights, axis=0, keepdims=True)
-        mixed = jnp.dot(values, weights.astype(jnp.bfloat16), preferred_element_type=jnp.float32)
-        acc[req, :, cols] = acc[req, :, cols] * shrink + mixed
+        stat[req, 1:2, cols] = total
+        acc[req, :, cols] = mixed
 
 
 def gather_kernel(
     side,
     owner_in, page_in, count, k_in, v_in, q_in, nk_in, nv_in,
-    k_near, v_near, k_far, v_far, q_all, t_all, acc, stat,
+    k_near, v_near, k_mid, v_mid, k_far, v_far, q_all, t_all, acc, stat,
     owner, page, table, vraw, qraw, nk, nv, send, recv, local,
 ):
     core, u, w = place(side)
@@ -75,7 +82,7 @@
     reach = k_near.shape[0] // 2
     heads_wide = q_all.shape[2] // 2
     shape = t_all.shape[1:]
-    middle = shape[1] // 2
+    lanes = shape[1] // 4
     slots = owner.shape[1]
     pages = k_in.shape[0]
     tokens = qraw.shape[0]
@@ -98,10 +105,10 @@
     pl.semaphore_wait(barrier, 4)
 
     def shard(kind, d):
-        near, far = ((k_near, k_far), (v_near, v_far))[kind]
+        near, mid, far = ((k_near, k_mid, k_far), (v_near, v_mid, v_far))[kind]
         if abs(d) <= reach:
             return near.at[d + reach]
-        return far.at[d % side - reach - 1]
+        return far.at[0] if abs(d) == half else mid.at[(reach - d) // side + 1]
 
     started = {}
     waited = set()
@@ -144,7 +151,7 @@
         copy.wait()
     line_at = lax.broadcasted_iota(jnp.int32, shape, 0)
     lane_at = lax.broadcasted_iota(jnp.int32, shape, 1)
-    filled = [jnp.zeros(shape, jnp.int32), jnp.full(shape, middle, jnp.int32)]
+    filled = [jnp.full(shape, g * lanes, jnp.int32) for g in range(3)]
     packed = jnp.zeros(shape, jnp.int32)
     for slot in range(slots):
         z, y = owner[0, slot] // side, lax.rem(owner[0, slot], side)
@@ -152,13 +159,20 @@
         cross = (1 - core) * y + core * z
         ahead = wrap(line - u + reach, side)
         listed = jnp.logical_and(line_at == cross, count[0] > slot)
-        for far in (0, 1):
-            hit = jnp.logical_and(listed, (ahead > 2 * reach) if far else (ahead <= 2 * reach))
-            spot = (ahead - far * (2 * reach + 1)) * pages + page[0, slot]
-            packed = jnp.where(jnp.logical_and(hit, lane_at == filled[far]), spot, packed)
-            filled[far] = filled[far] + jnp.where(hit, 1, 0)
-    packed = jnp.where(lane_at == middle - 1, filled[0], packed)
-    t_all[w] = jnp.where(lane_at == shape[1] - 1, filled[1] - middle, packed)
+        beyond = ahead - 2 * reach - 1
+        groups = (
+            (beyond < 0, ahead),
+            (jnp.logical_or(beyond == 0, beyond == 2), beyond // 2),
+            (beyond == 1, 0),
+        )
+        for g, (belongs, shard_at) in enumerate(groups):
+            hit = jnp.logical_and(listed, belongs)
+            spot = shard_at * pages + page[0, slot]
+            packed = jnp.where(jnp.logical_and(hit, lane_at == filled[g]), spot, packed)
+            filled[g] = filled[g] + jnp.where(hit, 1, 0)
+    for g in range(3):
+        packed = jnp.where(lane_at == (g + 1) * lanes - 1, filled[g] - g * lanes, packed)
+    t_all[w] = packed
     both(0, 3)
     fetch_q.wait()
     for j in range(GROUP):
@@ -180,7 +194,7 @@
 
     for copy in fresh:
         copy.wait()
-    accumulate(acc, stat, q_all, w, nk[...], jnp.transpose(nv[...]), causal=True)
+    accumulate(acc, stat, q_all, w, [(nk[...], jnp.transpose(nv[...]), None)], causal=True)
     receive((0, half - 1, 3))
     receive((1, half - 2, 3))
     to_scalars = fetch(7, t_all, table)
@@ -197,19 +211,30 @@
     own_k.wait()
     to_scalars.wait()
 
-    def listed_near(first, last):
-        @pl.loop(first * NEAR_SLOTS, last * NEAR_SLOTS)
-        def _(at):
-            req, k = at // NEAR_SLOTS, lax.rem(at, NEAR_SLOTS)
-            live = k < table[req, w, middle - 1]
-            spot = table[req, w, k]
-            line, page_at = spot // pages, lax.rem(spot, pages)
-            accumulate(acc, stat, q_all, req, k_near[line, page_at], v_near[line, page_at], live=live)
-
-    listed_near(0, half)
+    def listed(g, most, first, last, keys, values):
+        def one(req):
+            items = []
+            for k in range(most):
+                live = k < table[req, w, (g + 1) * lanes - 1]
+                spot = table[req, w, g * lanes + k]
+                shard_at, page_at = spot // pages, lax.rem(spot, pages)
+                items.append((keys[shard_at, page_at], values[shard_at, page_at], live))
+            accumulate(acc, stat, q_all, req, items)
+
+        if UNROLL:
+            for req in range(first, last):
+                one(req)
+        else:
+            pl.loop(first, last)(one)
+
+    listed(0, NEAR_SLOTS, 0, half, k_near, v_near)
     start(0, half - 1, 0)
     start(1, half - 1, 1)
-    listed_near(half, side)
+    listed(0, NEAR_SLOTS, half, side, k_near, v_near)
+    for dirn in (0, 1):
+        for kind in (0, 1):
+            receive((dirn, half - 2, kind))
+    listed(1, MID_SLOTS, 0, side, k_mid, v_mid)
     for key in started:
         receive(key)
     for copy in started.values():
@@ -228,21 +253,18 @@
 def gather_lines(owner, page, count, k, v, q, nk, nv, side):
     half = side // 2
     tokens = q.shape[0]
-    near, far = 2 * (half - 2) + 1, side - 2 * (half - 2) - 1
+    near = 2 * (half - 2) + 1
     return pl.pallas_call(
         functools.partial(gather_kernel, side),
         out_shape=[
-            pltpu.VMEM((near,) + k.shape, k.dtype),
-            pltpu.VMEM((near,) + v.shape, v.dtype),
-            pltpu.VMEM((far,) + k.shape, k.dtype),
-            pltpu.VMEM((far,) + v.shape, v.dtype),
+            *[pltpu.VMEM((n,) + a.shape, a.dtype) for n in (near, 2, 1) for a in (k, v)],
             pltpu.VMEM((side, HD, GROUP * tokens), q.dtype),
             pltpu.VMEM((side, side, 128), jnp.int32),
             pltpu.VMEM((side, HD, GROUP * tokens), jnp.float32),
             pltpu.VMEM((side, 2, GROUP * tokens), jnp.float32),
         ],
         in_specs=[HBM, HBM, SMEM] + [HBM] * 5,
-        out_specs=[VMEM] * 8,
+        out_specs=[VMEM] * 10,
         scratch_shapes=[
             pltpu.SMEM(owner.shape, owner.dtype),
             pltpu.SMEM(page.shape, page.dtype),
@@ -262,38 +284,35 @@
     )(in_hbm(owner), in_hbm(page), count, *[in_hbm(a) for a in (k, v, q, nk, nv)])
 
 
-def partial_kernel(side, table, k_near, v_near, k_far, v_far, q_all, acc_in, stat_in, acc, stat):
-    del acc_in, stat_in
+def partial_kernel(side, table, *refs):
+    shards, (q_all, _, _, acc, stat) = refs[:-5], refs[-5:]
     _, _, w = place(side)
-    pages = k_near.shape[1]
-    lanes = table.shape[2]
-    middle = lanes // 2
+    pages = shards[0].shape[1]
+    lanes = table.shape[2] // 4
 
     @pl.loop(0, side)
     def _(req):
-        @pl.loop(NEAR_SLOTS, jnp.maximum(table[req, w, middle - 1], NEAR_SLOTS))
-        def _(k):
-            spot = table[req, w, k]
-            line, page = spot // pages, lax.rem(spot, pages)
-            accumulate(acc, stat, q_all, req, k_near[line, page], v_near[line, page])
-
-        @pl.loop(0, table[req, w, lanes - 1])
-        def _(k):
-            spot = table[req, w, middle + k]
-            line, page = spot // pages, lax.rem(spot, pages)
-            accumulate(acc, stat, q_all, req, k_far[line, page], v_far[line, page])
-
-
-def partials(table, k_near, v_near, k_far, v_far, q_all, acc, stat, side):
+        for g, done in enumerate((NEAR_SLOTS, MID_SLOTS, 0)):
+            keys, values = shards[2 * g], shards[2 * g + 1]
+
+            @pl.loop(done, jnp.maximum(table[req, w, (g + 1) * lanes - 1], done))
+            def _(k):
+                spot = table[req, w, g * lanes + k]
+                shard_at, page_at = spot // pages, lax.rem(spot, pages)
+                accumulate(acc, stat, q_all, req, [(keys[shard_at, page_at], values[shard_at, page_at], None)])
+
+
+def partials(table, shards, q_all, acc, stat, side):
+    first = 2 + len(shards)
     return pl.pallas_call(
         functools.partial(partial_kernel, side),
         out_shape=[pltpu.VMEM(acc.shape, acc.dtype), pltpu.VMEM(stat.shape, stat.dtype)],
-        in_specs=[SMEM] + [VMEM] * 7,
+        in_specs=[SMEM] + [VMEM] * (first + 1),
         out_specs=[VMEM, VMEM],
-        input_output_aliases={6: 0, 7: 1},
+        input_output_aliases={first: 0, first + 1: 1},
         compiler_params=pltpu.CompilerParams(vmem_limit_bytes=16 << 20),
         name="partials",
-    )(table, k_near, v_near, k_far, v_far, q_all, acc, stat)
+    )(table, *shards, q_all, acc, stat)
 
 
 def return_kernel(side, accs, stats, out, outgoing, incoming, result, send, recv, xsend, xrecv, xlocal):
@@ -480,7 +499,7 @@
         new_values,
         side,
     )
-    acc_all, stat_all = partials(table, *shards, q_all, acc, stat, side)
+    acc_all, stat_all = partials(table, shards, q_all, acc, stat, side)
     return return_partials(acc_all, stat_all, side, peers)
 
 

time: 98.2 us -> 95.2 us (0.969)
  Pallas kernels: 96.7 us -> 93.7 us
    pallas_call x1, Pallas kernels: 28.2 us -> 25.6 us  [return_partials(): pl.pallas_call(functools.partial(return_kernel, side), out_shape=jax.Shap...]
where the time goes in v6:
time: 95.2 us; the launch traced here: 95.1 us
  Pallas kernels  93.7 us (98%)
    pallas_call x1, Pallas kernels, gather_lines(): pl.pallas_call(functools.partial(gather_kernel, side), out_shape=[*[pltpu...  65.3 us
    pallas_call x1, Pallas kernels, return_partials(): pl.pallas_call(functools.partial(return_kernel, side), out_shape=jax.Shap...  25.6 us
    pallas_call x1, Pallas kernels, partials(): pl.pallas_call(functools.partial(partial_kernel, side), out_shape=[pltpu....  2.79 us

profile of v6, /device:TPU:1, one launch (start us, length us, event | category | flops | bytes accessed | tf_op | source)
XLA Modules:
  0.0 95.1 jit_solution(12216883223752005202)
XLA Ops:
  0.7 65.3 %gather_lines.1 = (bf16[5,16,128,128]{3,2,1,0:T(8,128)(2,1)S(1)}, bf16[5,16,128,128]{3,2,1,0:T(8,128)(2,1)S(1)}, bf16[2,16,128,128]{3,2,1,0:T(8,128)(2,1)S(1)}, ...) custom-call(s32[1,16]{1,0:T(1,128)} %owner_in.1, ...), custom_call_target="tpu_custom_call" | custom-call | tf_op jit(solution)/shard_map/gather_lines/pallas_call | solution.py:257
  66.0 2.8 %partials.1 = (f32[8,128,1024]{2,1,0:T(8,128)S(1)}, f32[8,2,1024]{2,1,0:T(2,128)S(1)}) custom-call(s32[8,8,128]{2,1,0:T(8,128)S(1)} %get-tuple-element.17.table, bf16[5,16,128,128]{3,2,1,0:T(8,128)(2,1)S(1)} %get-tuple-element.18.refs_0_, bf16[5,16,128,128]{3,2,1,0:T(8,128)(2,1)S(1)} %get-tuple-element.19.refs_1_, ...), custom_call_target="tpu_custom_call", output_to_operand_aliasing={{0}: (8, {}), {1}: (9, {})} | custom-call | tf_op jit(solution)/shard_map/partials/pallas_call | solution.py:307
  68.8 25.6 %return_partials.1 = bf16[16,8192]{1,0:T(8,128)(2,1)S(1)} custom-call(f32[8,128,1024]{2,1,0:T(8,128)S(1)} %get-tuple-element.27.accs, f32[8,2,1024]{2,1,0:T(2,128)S(1)} %get-tuple-element.28.stats), custom_call_target="tpu_custom_call" | custom-call | tf_op jit(solution)/shard_map/return_partials/pallas_call | solution.py:456
  94.4 0.7 copy.15

commit v7 on v6

--- a/solution.py
+++ b/solution.py
@@ -15,7 +15,7 @@
 MESH = pl.DeviceIdType.MESH
 LOG2E = 1.4426950408889634
 FLOOR = -1e30
-NEAR_SLOTS = 3
+NEAR_SLOTS = 4
 MID_SLOTS = 2
 UNROLL = True
 
@@ -413,12 +413,12 @@
             final = item[0] / item[2]
             for j in range(part // tokens):
                 at = c * part // tokens + j
-                block = jnp.transpose(final[:, j * tokens : (j + 1) * tokens])
-                result[:, at * HD : (at + 1) * HD] = block.astype(result.dtype)
+                block = jnp.transpose(final[:, j * tokens : (j + 1) * tokens].astype(result.dtype))
+                result[:, at * HD : (at + 1) * HD] = block
         first, size = group[0] * part, len(group) * part
         here = slice(first, first + size)
         there = pl.ds(pl.multiple_of(me * width + first, size), size)
-        for hop in range(1, peers):
+        for hop in sorted(range(1, peers), key=lambda hop: abs(hop - peers // 2)):
             peer = lax.rem(me + hop, peers)
             copy = pltpu.make_async_remote_copy(
                 src_ref=result.at[pl.ds(pl.multiple_of(peer * share, share), share), here],
@@ -449,7 +449,7 @@
     half = side // 2
     rows = acc_all.shape[2]
     tokens = rows // GROUP
-    chunks = 4
+    chunks = 8
     width = GROUP * HD
     groups = len(exchange_groups(chunks))
     message = (2, chunks, half, HD + 8, rows // chunks)

time: 95.2 us -> 94.7 us (level)
  no operation moved by 1% of the time
where the time goes in v7:
time: 94.7 us; the launch traced here: 94.6 us
  Pallas kernels  93.2 us (98%)
    pallas_call x1, Pallas kernels, gather_lines(): pl.pallas_call(functools.partial(gather_kernel, side), out_shape=[*[pltpu...  65.3 us
    pallas_call x1, Pallas kernels, return_partials(): pl.pallas_call(functools.partial(return_kernel, side), out_shape=jax.Shap...  25.1 us
    pallas_call x1, Pallas kernels, partials(): pl.pallas_call(functools.partial(partial_kernel, side), out_shape=[pltpu....  2.78 us

profile of v7, /device:TPU:1, one launch (start us, length us, event | category | flops | bytes accessed | tf_op | source)
XLA Modules:
  0.0 94.6 jit_solution(16196838471735022695)
XLA Ops:
  0.7 65.3 %gather_lines.1 = (bf16[5,16,128,128]{3,2,1,0:T(8,128)(2,1)S(1)}, bf16[5,16,128,128]{3,2,1,0:T(8,128)(2,1)S(1)}, bf16[2,16,128,128]{3,2,1,0:T(8,128)(2,1)S(1)}, ...) custom-call(s32[1,16]{1,0:T(1,128)} %owner_in.1, ...), custom_call_target="tpu_custom_call" | custom-call | tf_op jit(solution)/shard_map/gather_lines/pallas_call | solution.py:257
  66.0 2.8 %partials.1 = (f32[8,128,1024]{2,1,0:T(8,128)S(1)}, f32[8,2,1024]{2,1,0:T(2,128)S(1)}) custom-call(s32[8,8,128]{2,1,0:T(8,128)S(1)} %get-tuple-element.17.table, bf16[5,16,128,128]{3,2,1,0:T(8,128)(2,1)S(1)} %get-tuple-element.18.refs_0_, bf16[5,16,128,128]{3,2,1,0:T(8,128)(2,1)S(1)} %get-tuple-element.19.refs_1_, ...), custom_call_target="tpu_custom_call", output_to_operand_aliasing={{0}: (8, {}), {1}: (9, {})} | custom-call | tf_op jit(solution)/shard_map/partials/pallas_call | solution.py:307
  68.8 25.1 %return_partials.1 = bf16[16,8192]{1,0:T(8,128)(2,1)S(1)} custom-call(f32[8,128,1024]{2,1,0:T(8,128)S(1)} %get-tuple-element.27.accs, f32[8,2,1024]{2,1,0:T(2,128)S(1)} %get-tuple-element.28.stats), custom_call_target="tpu_custom_call" | custom-call | tf_op jit(solution)/shard_map/return_partials/pallas_call | solution.py:456
  93.9 0.7 copy.15

commit v8 on v7

--- a/solution.py
+++ b/solution.py
@@ -388,7 +388,7 @@
         flights[dirn, c, k].wait_recv()
         return unpack(incoming.at[dirn, c, k])
 
-    starts = [(c, dirn) for c in range(chunks) for dirn in (0, 1)]
+    starts = sorted(((c, dirn) for c in range(chunks) for dirn in (0, 1)), key=lambda at: -far(at[1], at[0]))
     for c, dirn in starts:
         pack(outgoing.at[dirn, c, 0], mine((1, -1)[dirn] * far(dirn, c), c))
     pl.semaphore_wait(barrier, 1 + peers)

time: 94.7 us -> 93.7 us (0.989)
  Pallas kernels: 93.2 us -> 92.1 us
where the time goes in v8:
time: 93.7 us; the launch traced here: 93.4 us
  Pallas kernels  92.1 us (98%)
    pallas_call x1, Pallas kernels, gather_lines(): pl.pallas_call(functools.partial(gather_kernel, side), out_shape=[*[pltpu...  65.3 us
    pallas_call x1, Pallas kernels, return_partials(): pl.pallas_call(functools.partial(return_kernel, side), out_shape=jax.Shap...  24.9 us

profile of v8, /device:TPU:1, one launch (start us, length us, event | category | flops | bytes accessed | tf_op | source)
XLA Modules:
  0.0 93.4 jit_solution(14300119846702275548)
XLA Ops:
  0.7 65.3 %gather_lines.1 = (bf16[5,16,128,128]{3,2,1,0:T(8,128)(2,1)S(1)}, bf16[5,16,128,128]{3,2,1,0:T(8,128)(2,1)S(1)}, bf16[2,16,128,128]{3,2,1,0:T(8,128)(2,1)S(1)}, ...) custom-call(s32[1,16]{1,0:T(1,128)} %owner_in.1, ...), custom_call_target="tpu_custom_call" | custom-call | tf_op jit(solution)/shard_map/gather_lines/pallas_call | solution.py:257
  66.0 1.9 %partials.1 = (f32[8,128,1024]{2,1,0:T(8,128)S(1)}, f32[8,2,1024]{2,1,0:T(2,128)S(1)}) custom-call(s32[8,8,128]{2,1,0:T(8,128)S(1)} %get-tuple-element.17.table, bf16[5,16,128,128]{3,2,1,0:T(8,128)(2,1)S(1)} %get-tuple-element.18.refs_0_, bf16[5,16,128,128]{3,2,1,0:T(8,128)(2,1)S(1)} %get-tuple-element.19.refs_1_, ...), custom_call_target="tpu_custom_call", output_to_operand_aliasing={{0}: (8, {}), {1}: (9, {})} | custom-call | tf_op jit(solution)/shard_map/partials/pallas_call | solution.py:307
  67.9 24.9 %return_partials.1 = bf16[16,8192]{1,0:T(8,128)(2,1)S(1)} custom-call(f32[8,128,1024]{2,1,0:T(8,128)S(1)} %get-tuple-element.27.accs, f32[8,2,1024]{2,1,0:T(2,128)S(1)} %get-tuple-element.28.stats), custom_call_target="tpu_custom_call" | custom-call | tf_op jit(solution)/shard_map/return_partials/pallas_call | solution.py:456
  92.7 0.7 copy.15
